TPU v7x, 512 devices: a whole 4x8x8 slice. The times are simulated.
512 devices in a mesh: row: 4 (over x), col: 32 (over z_lo, y, core), depth: 4 (over z_hi).
Axes of the slice: x: 4, y: 8, z: 8 (z_hi: 4, z_lo: 2; z = z_hi * 2 + z_lo), core: 2. Of those that a mesh axis runs over, the one named last changes fastest.
Arguments:
- left_slab: bfloat16 [4096, 4096], P(None, ('col', 'depth')), may hold values from -6 to 6
- right_vectors: bfloat16 [65536, 4096], P('col', 'depth'), may hold values from -0.09375 to 0.09375
- pair_weight: float32 [4096], P(('col', 'depth')), may hold values from -6 to 6
- eigenvalue: float32 [4096], P(('col', 'depth')), may hold values from -2 to 2
- pair_order: int32 [4096], replicated, may hold values from 0 to 4095, each once
- row_offset: int32 [1], replicated, may hold values from 0 to 3072
Outputs:
- grads: bfloat16 [3, 1024, 65536], P(None, 'row', ('col', 'depth'))
Inputs may be any that keep to these rules, and one draw needn't show every extreme that they name: `pair_order`: each of 0 to 4095 appears exactly once.
All inputs are finite; a program needn't handle non-finite values.
Results may differ from a plain program's by a relative error of at most 0.023.
Values may be sent and summed in bfloat16 or wider, within the bound.
No kernel may reach another device: no remote copies, remote signals or barrier semaphores. Data moves between devices by JAX's collectives and lax.ppermute only.
A program may use at most 64 MiB of HBM per device.

v0:
```python
import jax
import jax.numpy as jnp
from jax import lax
from jax.sharding import PartitionSpec as P

P_SIZE = 1024


def scale_rows(left, weight, lam, columns):
    picked = jnp.take(left, columns, axis=1).astype(jnp.float32)
    w_pick = jnp.take(weight, columns)
    l_pick = jnp.take(lam, columns)
    powers = jnp.stack([w_pick, w_pick * l_pick, w_pick * l_pick * l_pick])
    scaled = (picked[None, :, :] * powers[:, None, :]).astype(jnp.bfloat16)
    return scaled.reshape(3 * left.shape[0], columns.shape[0])


def on_device(left_slab, right_vectors, pair_weight, eigenvalue, pair_order, row_offset):
    panel_rows = P_SIZE // lax.axis_size("row")
    start = row_offset[0] + lax.axis_index("row") * panel_rows
    local_rows = lax.dynamic_slice_in_dim(left_slab, start, panel_rows, 0)
    pieces = (local_rows, pair_weight[None, :], eigenvalue[None, :])
    left, weight, lam = (
        lax.all_gather(pieces[0], ("col", "depth"), axis=1, tiled=True),
        lax.all_gather(pieces[1].astype(jnp.bfloat16), ("col", "depth"), axis=1, tiled=True).astype(
            jnp.float32
        ),
        lax.all_gather(pieces[2].astype(jnp.bfloat16), ("col", "depth"), axis=1, tiled=True).astype(
            jnp.float32
        ),
    )
    weight = weight[0]
    lam = lam[0]
    group_width = right_vectors.shape[1]
    members = lax.dynamic_slice_in_dim(
        pair_order, lax.axis_index("depth") * group_width, group_width, 0
    )
    scaled = scale_rows(left, weight, lam, members)
    partial_sums = lax.dot_general(
        scaled, right_vectors, (((1,), (1,)), ((), ())), preferred_element_type=jnp.float32
    )
    partial_sums = partial_sums.reshape(3, panel_rows, right_vectors.shape[0])
    total = lax.psum_scatter(
        partial_sums.astype(jnp.bfloat16), "depth", scatter_dimension=2, tiled=True
    )
    return total


def solution(mesh):
    in_specs = (
        P(None, ("col", "depth")),
        P("col", "depth"),
        P(("col", "depth")),
        P(("col", "depth")),
        P(),
        P(),
    )
    out_specs = P(None, "row", ("col", "depth"))
    return jax.shard_map(
        on_device, mesh=mesh, in_specs=in_specs, out_specs=out_specs, check_vma=False
    )
```

profile of v0, /device:TPU:1, one launch (start us, length us, event | category | flops | bytes accessed | tf_op | source)
XLA Modules:
  0.0 726.9 jit_solution(14187154908876779473)
XLA Ops:
  6.5 0.0 copy-start
  6.5 0.0 all-gather.4.cloned.1.call-start
  7.2 0.3 copy-done
  7.5 0.7 constant_dynamic-slice_fusion
  8.2 0.0 all-gather.4.cloned.1.call-update
  8.2 0.0 reduce-scatter.2.cloned.1.call-start
  8.3 0.7 convert_element_type.30
  8.9 0.7 convert_element_type.32
  9.6 1.3 dynamic-slice
  11.5 0.2 dynamic-update-slice.1
  11.8 0.2 dynamic-update-slice
  12.0 523.1 %all-reduce.2 = (bf16[4096]{0:T(1024)(128)(2,1)S(1)}, bf16[4096]{0:T(1024)(128)(2,1)S(1)}) all-reduce(bf16[4096]{0:T(1024)(128)(2,1)S(1)} %dynamic-update-slice.1, bf16[4096]{0:T(1024)(128)(2,1)S(1)} %dynamic-update-slice), channel_id=3, replica_groups=mesh['row'=4,'col'=32,'depth'=4] {'col','depth'}, use_global_device_ids=true, to_apply=%add.1 | all-reduce | flops 8192 | bytes 32768
  535.1 0.7 fusion.7
  535.7 6.1 gather_fusion.2
  541.9 6.2 gather_fusion.1
  548.1 0.7 broadcast_select_fusion.1
  548.8 0.0 all-gather.4.cloned.1.call-done
  548.8 5.3 gather_fusion
  554.2 0.2 convert_bitcast_fusion
  554.4 0.3 copy.8
  554.7 7.0 fusion.2
  561.7 0.0 reduce-scatter.2.cloned.1.call-update
  561.8 158.3 %reduce-scatter.2.cloned.1.call-done = bf16[3,256,512]{2,1,0:T(8,128)(2,1)} async-done(((bf16[3,256,2048]{2,1,0:T(8,128)(2,1)}), bf16[3,256,512]{2,1,0:T(8,128)(2,1)}) %reduce-scatter.2.cloned.1.call-update) | async-done | bytes 786448 | tf_op jit(solution)/shard_map/reduce_scatter | solution.py:43
  (6 shorter events, 0.0 us)
Async XLA Ops:
  6.5 1.0 copy-start
  6.5 542.3 %all-gather.4.cloned.1.call-start = ((), (), s32[]{:S(2)}) async-start(), calls=%async_computation.1 | async-start | bytes 2113536 | tf_op jit(solution)/shard_map/all_gather | solution.py:24
  8.2 711.9 %reduce-scatter.2.cloned.1.call-start = ((), (), s32[]{:S(2)}) async-start(), calls=%async_computation.2 | async-start | bytes 3932160 | tf_op jit(solution)/shard_map/reduce_scatter | solution.py:43
Sparse Core Ops, SparseCore 0:
  9.5 368.3 all-gather.3
  561.9 158.1 reduce-scatter.1
where the time goes:
time: 727 us
  blocking collectives  523 us (72%)
  waiting for transfers between devices  158 us (22%)
  local copies, waits for them, and re-layouts  20.7 us (3%)
  between operations  14.8 us (2%)
    unnamed x1, blocking collectives  523 us
    reduce_scatter x1, waiting for transfers between devices, on_device(): lax.psum_scatter(partial_sums.astype(jnp.bfloat16), 'depth', scatter_dime...  158 us
  transfers between devices with their start and end apart: 2, of which 1 were waited for; matrix products, arithmetic and copies ran while one was open for 2% of the time, Pallas kernels for 0%

commit v1 on v0

v1 whole, which is shorter than its diff:
```python
import functools

import jax
import jax.numpy as jnp
from jax import lax
from jax.experimental import pallas as pl
from jax.experimental.pallas import tpu as pltpu
from jax.sharding import Mesh, PartitionSpec as P

P_SIZE = 1024
LANES = 128
TILE = 512
BLOCK = 256


def everyone(x, axes):
    n = lax.axis_size(axes)
    return lax.all_to_all(jnp.broadcast_to(x[None], (n,) + x.shape), axes, 0, 0)


def shifted(x, axis, by):
    n = lax.axis_size(axis)
    return lax.ppermute(x, axis, [(i, (i + by) % n) for i in range(n)])


def order_kernel(core_ref, order_ref, own_ref, other_ref, s_ref, lt_ref, mt_ref):
    width = 32

    @pl.when(pl.program_id(0) == 0)
    def _():
        for h, src in enumerate((own_ref, other_ref)):
            for a in range(2):
                for q in range(16):
                    blk = src[4 * q:4 * q + 4, a * width:(a + 1) * width, :].reshape(LANES, LANES)
                    lt_ref[h, a * LANES:(a + 1) * LANES, q * LANES:(q + 1) * LANES] = blk.T
            mt_ref[h] = src[:, 2 * width, :].astype(jnp.float32).T.astype(jnp.bfloat16)

    e = order_ref[...]
    j = e & 31
    q = e >> 5
    core = (q >> 2) & 1
    d = ((q >> 3) & 7) * 8 + (q >> 6) * 4 + (q & 3)
    mine = core == core_ref[0]
    storage = jnp.where(mine, d * width + j, 2048 + d * width + j)
    acc = jnp.zeros((2 * LANES, TILE), jnp.float32)
    rows = lax.broadcasted_iota(jnp.int32, (BLOCK, TILE), 0)
    for h in range(2):
        for b in range(2048 // BLOCK):
            hot = jnp.where(rows == storage - (h * 2048 + b * BLOCK), 1.0, 0.0).astype(jnp.bfloat16)
            acc += jnp.dot(lt_ref[h, :, b * BLOCK:(b + 1) * BLOCK], hot, preferred_element_type=jnp.float32)
    src_rows = lax.broadcasted_iota(jnp.int32, (64, TILE), 0)
    d_own = jnp.where(mine, d, -1)
    d_other = jnp.where(mine, -1, d)
    picked = jnp.dot(mt_ref[0], jnp.where(src_rows == d_own, 1.0, 0.0).astype(jnp.bfloat16), preferred_element_type=jnp.float32)
    picked += jnp.dot(mt_ref[1], jnp.where(src_rows == d_other, 1.0, 0.0).astype(jnp.bfloat16), preferred_element_type=jnp.float32)
    at_j = lax.broadcasted_iota(jnp.int32, (width, TILE), 0) == j
    parts = [
        jnp.sum(jnp.where(at_j, picked[i * width:(i + 1) * width], 0.0), axis=0, keepdims=True) for i in range(4)
    ]
    w = parts[0] + parts[1]
    lam = parts[2] + parts[3]
    s_ref[0, 0] = (acc * w).astype(jnp.bfloat16)
    s_ref[0, 1] = (acc * (w * lam)).astype(jnp.bfloat16)
    s_ref[0, 2] = (acc * (w * lam * lam)).astype(jnp.bfloat16)


def ordered_powers(core, pair_order, own, other):
    k = pair_order.shape[0]
    per_group = k // 4
    steps = per_group // TILE
    return pl.pallas_call(
        order_kernel,
        grid=(k // TILE,),
        in_specs=[
            pl.BlockSpec(memory_space=pltpu.SMEM),
            pl.BlockSpec((1, TILE), lambda t: (0, t)),
            pl.BlockSpec(own.shape, lambda t: (0, 0, 0)),
            pl.BlockSpec(own.shape, lambda t: (0, 0, 0)),
        ],
        out_specs=pl.BlockSpec((1, 3, 2 * LANES, TILE), lambda t: (t // steps, 0, 0, t % steps)),
        out_shape=jax.ShapeDtypeStruct((4, 3, 2 * LANES, per_group), jnp.bfloat16),
        scratch_shapes=[pltpu.VMEM((2, 2 * LANES, 2048), jnp.bfloat16), pltpu.VMEM((2, LANES, 64), jnp.bfloat16)],
        compiler_params=pltpu.CompilerParams(vmem_limit_bytes=40 * 2**20),
        cost_estimate=pl.CostEstimate(flops=2 * k * k * 256, bytes_accessed=12 * 2**20, transcendentals=0),
    )(core[None], pair_order[None], own, other)


def contract_kernel(at_ref, s_ref, own_ref, na_ref, nb_ref, a1, b1, a2, b2, a3, b3, o_ref):
    r, d = at_ref[0], at_ref[1]
    near = ((na_ref, nb_ref), (a1, b1), (a2, b2), (a3, b3))
    before, across, after = (d + 3) % 4, (d + 2) % 4, (d + 1) % 4
    nt = (((1,), (1,)), ((), ()))
    for pair in range(2):
        ts = (2 * pair, 2 * pair + 1)
        qs = [(r - t + 4) % 4 for t in ts]
        for m in range(3):
            acc = None
            for g, get in (
                (d, lambda t, q: own_ref[0, q]),
                (before, lambda t, q: near[t][0][0]),
                (after, lambda t, q: near[t][0][1]),
                (across, lambda t, q: near[t][1][...]),
            ):
                rhs = jnp.concatenate([get(t, q) for t, q in zip(ts, qs)], axis=0)
                part = lax.dot_general(s_ref[g, m], rhs, nt, preferred_element_type=jnp.float32)
                acc = part if acc is None else acc + part
            out = acc.astype(jnp.bfloat16)
            for n, q in enumerate(qs):
                o_ref[m, :, pl.ds(pl.multiple_of(q * LANES, LANES), LANES)] = out[:, n * LANES:(n + 1) * LANES]


def contract(at, s, rv, near, far):
    vm = pl.BlockSpec(memory_space=pltpu.VMEM)
    flat = [v for ab in (near, *far) for v in ab]
    grid_spec = pltpu.PrefetchScalarGridSpec(
        num_scalar_prefetch=1,
        grid=(1,),
        in_specs=[
            pl.BlockSpec(s.shape, lambda i, at: (0, 0, 0, 0)),
            pl.BlockSpec((1,) + rv.shape[1:], lambda i, at: (at[1], 0, 0, 0)),
        ] + [pl.BlockSpec(v.shape, lambda i, at, n=v.ndim: (0,) * n) for v in flat],
        out_specs=pl.BlockSpec((3, 256, 512), lambda i, at: (0, 0, 0)),
    )
    return pl.pallas_call(
        contract_kernel,
        grid_spec=grid_spec,
        out_shape=jax.ShapeDtypeStruct((3, 256, 512), jnp.bfloat16),
        compiler_params=pltpu.CompilerParams(vmem_limit_bytes=48 * 2**20),
        cost_estimate=pl.CostEstimate(flops=2 * 768 * 4096 * 512, bytes_accessed=11 * 2**20, transcendentals=0),
    )(at, s, rv, *flat)


def split(v):
    hi = lax.reduce_precision(v, 8, 7)
    return [hi.astype(jnp.bfloat16), (v - hi).astype(jnp.bfloat16)]


def on_device(left_slab, right_vectors, pair_weight, eigenvalue, pair_order, row_offset):
    n_depth, n_row = lax.axis_size("depth"), lax.axis_size("row")
    r, d = lax.axis_index("row"), lax.axis_index("depth")
    panel_rows = P_SIZE // n_row
    cols, group = right_vectors.shape
    quarter = cols // n_depth // n_row
    rv = right_vectors.reshape(n_depth, n_row, quarter, group)

    def piece(by):
        return lax.dynamic_slice(rv, ((d + by) % n_depth, r, 0, 0), (1, 1, quarter, group)).reshape(quarter, group)

    z1 = shifted(piece(1), "depth", 1)
    z3 = shifted(piece(3), "depth", 3)
    z2 = shifted(piece(2), "depth", 2)
    near = jnp.stack([z1, z3])
    far = [(shifted(near, "row", t), shifted(z2, "row", t)) for t in (1, 2, 3)]

    start = row_offset[0] + r * panel_rows
    mine = lax.dynamic_slice_in_dim(left_slab.T, start, panel_rows, 1)
    scal = jnp.concatenate(split(pair_weight) + split(eigenvalue))
    scal = jnp.broadcast_to(scal[None], (8, LANES))
    mine = jnp.concatenate([mine[:, :LANES], mine[:, LANES:], scal], axis=0)
    by_z = everyone(mine, ("zlo", "depth"))
    by_y = everyone(by_z, "y").reshape(64, 72, LANES)
    other = shifted(by_y, "core", 1)
    s = ordered_powers(lax.axis_index("core"), pair_order, by_y, other)
    return contract(jnp.stack([r, d]), s, rv, (near, z2), far)


def solution(mesh):
    fine = Mesh(mesh.devices.reshape(4, 2, 8, 2, 4), ("row", "zlo", "y", "core", "depth"))
    col = ("zlo", "y", "core")
    all_k = col + ("depth",)
    in_specs = (P(None, all_k), P(col, "depth"), P(all_k), P(all_k), P(), P())
    return jax.shard_map(on_device, mesh=fine, in_specs=in_specs, out_specs=P(None, "row", all_k), check_vma=False)
```

time: 727 us -> 144 us (0.20)
  the two profiles are of different devices: /device:TPU:1 before, /device:TPU:3 now
where the time goes in v1:
time: 144 us
  blocking collectives  52.1 us (36%)
  starting transfers between devices  33.8 us (23%)
  waiting for transfers between devices  28.2 us (20%)
  Pallas kernels  21.6 us (15%)
  local copies, waits for them, and re-layouts  5.07 us (4%)
  other arithmetic  1.92 us (1%)
    all_to_all x2, blocking collectives, everyone(): return lax.all_to_all(jnp.broadcast_to(x[None], (n,) + x.shape), axes, 0, 0)  52.1 us
    ppermute x10, starting transfers between devices, shifted(): return lax.ppermute(x, axis, [(i, (i + by) % n) for i in range(n)])  33.8 us
    ppermute x10, waiting for transfers between devices, shifted(): return lax.ppermute(x, axis, [(i, (i + by) % n) for i in range(n)])  28.2 us
    pallas_call x1, Pallas kernels, ordered_powers(): pl.pallas_call(order_kernel, grid=(k // TILE,), in_specs=[pl.BlockSpec(me...  13.6 us
    pallas_call x1, Pallas kernels, contract(): pl.pallas_call(contract_kernel, grid_spec=grid_spec, out_shape=jax.ShapeD...  8.03 us
    unnamed x6, local copies, waits for them, and re-layouts  2.91 us
  transfers between devices with their start and end apart: 10, of which 4 were waited for; matrix products, arithmetic and copies ran while one was open for 2% of the time, Pallas kernels for 9%

profile of v1, /device:TPU:3, one launch (start us, length us, event | category | flops | bytes accessed | tf_op | source)
XLA Modules:
  0.0 143.6 jit_solution(13772368757022901456)
XLA Ops:
  0.0 0.0 copy-start
  0.0 0.0 copy-start.2
  0.7 0.3 copy-done
  1.0 0.1 dynamic-slice_bitcast_fusion.3
  1.1 0.7 reduce-precision_convert_fusion
  1.7 0.1 pad_maximum_fusion.2
  1.9 16.9 %all_to_all.10 = bf16[8,72,128]{2,1,0:T(8,128)(2,1)S(1)} all-to-all(bf16[8,72,128]{2,1,0:T(8,128)(2,1)S(1)} %broadcast_in_dim.13), channel_id=1, replica_groups=mesh['row'=4,'zlo'=2,'y'=8,'core'=2,'depth'=4] {'zlo','depth'}, dimensions={0} | all-to-all | bytes 294912 | tf_op jit(solution)/shard_map/all_to_all | solution.py:18
  18.8 0.2 broadcast_in_dim.28
  18.9 35.2 %all_to_all.11 = bf16[8,8,72,128]{3,2,1,0:T(8,128)(2,1)S(1)} all-to-all(bf16[8,8,72,128]{3,2,1,0:T(8,128)(2,1)S(1)} %broadcast_in_dim.28), channel_id=1, replica_groups=mesh['row'=4,'zlo'=2,'y'=8,'core'=2,'depth'=4] {'y'}, dimensions={0} | all-to-all | bytes 2359296 | tf_op jit(solution)/shard_map/all_to_all | solution.py:18
  54.1 5.8 %collective-permute-start = (bf16[64,72,128]{2,1,0:T(8,128)(2,1)S(1)}, bf16[64,72,128]{2,1,0:T(8,128)(2,1)S(1)}, u32[]{:S(2)}, u32[]{:S(2)}) collective-permute-start(bf16[64,72,128]{2,1,0:T(8,128)(2,1)S(1)} %bitcast.18), channel_id=1, source_target_pairs={{0,4},{4,0},{1,5},{5,1},{2,6},{6,2},{3,7},{7,3},{8,12},{12,8},{9,1... | collective-permute-start | bytes 3538952 | tf_op jit(solution)/shard_map/ppermute | solution.py:23
  60.0 1.9 %dynamic-slice_bitcast_fusion = (bf16[128,1024]{1,0:T(8,128)(2,1)S(1)}, bf16[128,1024]{1,0:T(8,128)(2,1)}, bf16[128,1024]{1,0:T(8,128)(2,1)S(1)}) fusion(bf16[4,4,128,1024]{3,2,1,0:T(8,128)(2,1)} %bitcast.21, s32[]{:T(128)S(6)} %select_n.39, s32[]{:T(128)S(6)} %select_n.35, s32[]{:T(128)S(6)} %select_n.37, s32[]{:T(128)S(6)} %select_n.34), kind=kLoop, calls=%fused_computation.1 | loop fusion | bytes 1572880 | tf_op jit(solution)/shard_map/reshape | solution.py:147
  61.9 3.8 %collective-permute-start.3 = (bf16[128,1024]{1,0:T(8,128)(2,1)S(1)}, bf16[128,1024]{1,0:T(8,128)(2,1)S(1)}, u32[]{:S(2)}, u32[]{:S(2)}) collective-permute-start(bf16[128,1024]{1,0:T(8,128)(2,1)S(1)} %get-tuple-element.5), channel_id=1, source_target_pairs={{0,2},{1,3},{2,0},{3,1},{4,6},{5,7},{6,4},{7,5},{8,10},{9,11},{10,... | collective-permute-start | bytes 786440 | tf_op jit(solution)/shard_map/ppermute | solution.py:23
  65.7 3.9 %collective-permute-start.2 = (bf16[128,1024]{1,0:T(8,128)(2,1)}, bf16[128,1024]{1,0:T(8,128)(2,1)}, u32[]{:S(2)}, u32[]{:S(2)}) collective-permute-start(bf16[128,1024]{1,0:T(8,128)(2,1)} %get-tuple-element.6), channel_id=1, source_target_pairs={{0,3},{1,0},{2,1},{3,2},{4,7},{5,4},{6,5},{7,6},{8,11},{9,8},{10,9... | collective-permute-start | bytes 786440 | tf_op jit(solution)/shard_map/ppermute | solution.py:23
  69.6 2.3 %collective-permute-start.1 = (bf16[128,1024]{1,0:T(8,128)(2,1)S(1)}, bf16[128,1024]{1,0:T(8,128)(2,1)}, u32[]{:S(2)}, u32[]{:S(2)}) collective-permute-start(bf16[128,1024]{1,0:T(8,128)(2,1)S(1)} %get-tuple-element.7), channel_id=1, source_target_pairs={{0,1},{1,2},{2,3},{3,0},{4,5},{5,6},{6,7},{7,4},{8,9},{9,10},{10,1... | collective-permute-start | bytes 786440 | tf_op jit(solution)/shard_map/ppermute | solution.py:23
  71.9 7.1 %collective-permute-done.3.nb_ref = bf16[128,1024]{1,0:T(8,128)(2,1)S(1)} collective-permute-done((bf16[128,1024]{1,0:T(8,128)(2,1)S(1)}, bf16[128,1024]{1,0:T(8,128)(2,1)S(1)}, u32[]{:S(2)}, u32[]{:S(2)}) %collective-permute-start.3) | collective-permute-done | bytes 262176 | tf_op jit(solution)/shard_map/ppermute | solution.py:23
  79.0 3.1 %collective-permute-start.5 = (bf16[128,1024]{1,0:T(8,128)(2,1)S(1)}, bf16[128,1024]{1,0:T(8,128)(2,1)S(1)}, u32[]{:S(2)}, u32[]{:S(2)}) collective-permute-start(bf16[128,1024]{1,0:T(8,128)(2,1)S(1)} %collective-permute-done.3.nb_ref), channel_id=1, source_target_pairs={{0,128},{128,256},{256,384},{384,0},{1,129},{129,257},{257,385},{3... | collective-permute-start | bytes 786440 | tf_op jit(solution)/shard_map/ppermute | solution.py:23
  82.1 0.1 pad_add_fusion.at_ref
  82.2 9.4 %collective-permute-done.2 = bf16[128,1024]{1,0:T(8,128)(2,1)} collective-permute-done((bf16[128,1024]{1,0:T(8,128)(2,1)}, bf16[128,1024]{1,0:T(8,128)(2,1)}, u32[]{:S(2)}, u32[]{:S(2)}) %collective-permute-start.2) | collective-permute-done | bytes 262176 | tf_op jit(solution)/shard_map/ppermute | solution.py:23
  91.6 0.0 collective-permute-done.1
  91.6 1.1 pad_maximum_fusion.na_ref
  92.7 3.1 %collective-permute-start.4 = (bf16[2,128,1024]{2,1,0:T(8,128)(2,1)S(1)}, bf16[2,128,1024]{2,1,0:T(8,128)(2,1)S(1)}, u32[]{:S(2)}, u32[]{:S(2)}) collective-permute-start(bf16[2,128,1024]{2,1,0:T(8,128)(2,1)S(1)} %pad_maximum_fusion.na_ref), channel_id=1, source_target_pairs={{0,128},{128,256},{256,384},{384,0},{1,129},{129,257},{257,385},{3... | collective-permute-start | bytes 1572872 | tf_op jit(solution)/shard_map/ppermute | solution.py:23
  95.8 2.7 %collective-permute-start.6 = (bf16[2,128,1024]{2,1,0:T(8,128)(2,1)S(1)}, bf16[2,128,1024]{2,1,0:T(8,128)(2,1)S(1)}, u32[]{:S(2)}, u32[]{:S(2)}) collective-permute-start(bf16[2,128,1024]{2,1,0:T(8,128)(2,1)S(1)} %pad_maximum_fusion.na_ref), channel_id=1, source_target_pairs={{0,256},{128,384},{256,0},{384,128},{1,257},{129,385},{257,1},{385... | collective-permute-start | bytes 1572872 | tf_op jit(solution)/shard_map/ppermute | solution.py:23
  98.5 3.8 %collective-permute-start.8 = (bf16[2,128,1024]{2,1,0:T(8,128)(2,1)S(1)}, bf16[2,128,1024]{2,1,0:T(8,128)(2,1)S(1)}, u32[]{:S(2)}, u32[]{:S(2)}) collective-permute-start(bf16[2,128,1024]{2,1,0:T(8,128)(2,1)S(1)} %pad_maximum_fusion.na_ref), channel_id=1, source_target_pairs={{0,384},{128,0},{256,128},{384,256},{1,385},{129,1},{257,129},{385... | collective-permute-start | bytes 1572872 | tf_op jit(solution)/shard_map/ppermute | solution.py:23
  102.3 0.0 collective-permute-done.5.b1
  102.3 2.2 %collective-permute-start.7 = (bf16[128,1024]{1,0:T(8,128)(2,1)S(1)}, bf16[128,1024]{1,0:T(8,128)(2,1)S(1)}, u32[]{:S(2)}, u32[]{:S(2)}) collective-permute-start(bf16[128,1024]{1,0:T(8,128)(2,1)S(1)} %collective-permute-done.3.nb_ref), channel_id=1, source_target_pairs={{0,256},{128,384},{256,0},{384,128},{1,257},{129,385},{257,1},{385... | collective-permute-start | bytes 786440 | tf_op jit(solution)/shard_map/ppermute | solution.py:23
  104.5 0.0 collective-permute-done.other_ref
  104.6 3.0 %collective-permute-start.9 = (bf16[128,1024]{1,0:T(8,128)(2,1)S(1)}, bf16[128,1024]{1,0:T(8,128)(2,1)S(1)}, u32[]{:S(2)}, u32[]{:S(2)}) collective-permute-start(bf16[128,1024]{1,0:T(8,128)(2,1)S(1)} %collective-permute-done.3.nb_ref), channel_id=1, source_target_pairs={{0,384},{128,0},{256,128},{384,256},{1,385},{129,1},{257,129},{385... | collective-permute-start | bytes 786440 | tf_op jit(solution)/shard_map/ppermute | solution.py:23
  107.6 0.0 copy-done.2
  107.6 13.6 %shard_map.64.s_ref = bf16[4,3,256,1024]{3,2,1,0:T(8,128)(2,1)S(1)} custom-call(s32[1]{0:T(128)} %bitcast.2.core_ref, s32[1,4096]{1,0:T(1,128)S(1)} %bitcast.20, bf16[64,72,128]{2,1,0:T(8,128)(2,1)S(1)} %bitcast.19, bf16[64,72,128]{2,1,0:T(8,128)(2,1)S(1)} %collective-permute-done.other_ref), custom_call_target="tpu_custom_call" | custom-call | flops 8589934592 | bytes 12582912 | tf_op jit(solution)/shard_map/pallas_call | solution.py:71
  121.1 0.0 copy-start.1
  121.2 2.6 %copy-done.1 = bf16[4,3,256,1024]{3,2,1,0:T(8,128)(2,1)} copy-done((bf16[4,3,256,1024]{3,2,1,0:T(8,128)(2,1)}, bf16[4,3,256,1024]{3,2,1,0:T(8,128)(2,1)S(1)}, u32[]{:S(2)}) %copy-start.1) | copy-done | bytes 6291480
  123.8 5.0 %collective-permute-done.7.b2 = bf16[128,1024]{1,0:T(8,128)(2,1)S(1)} collective-permute-done((bf16[128,1024]{1,0:T(8,128)(2,1)S(1)}, bf16[128,1024]{1,0:T(8,128)(2,1)S(1)}, u32[]{:S(2)}, u32[]{:S(2)}) %collective-permute-start.7) | collective-permute-done | bytes 262176 | tf_op jit(solution)/shard_map/ppermute | solution.py:23
  128.8 6.7 %collective-permute-done.9.b3 = bf16[128,1024]{1,0:T(8,128)(2,1)S(1)} collective-permute-done((bf16[128,1024]{1,0:T(8,128)(2,1)S(1)}, bf16[128,1024]{1,0:T(8,128)(2,1)S(1)}, u32[]{:S(2)}, u32[]{:S(2)}) %collective-permute-start.9) | collective-permute-done | bytes 262176 | tf_op jit(solution)/shard_map/ppermute | solution.py:23
  135.5 0.0 collective-permute-done.4.a1
  135.5 0.0 collective-permute-done.6.a2
  135.5 0.0 collective-permute-done.8.a3
  135.5 8.0 %shard_map.65 = bf16[3,256,512]{2,1,0:T(8,128)(2,1)} custom-call(s32[2]{0:T(128)S(1)} %pad_add_fusion.at_ref, bf16[4,3,256,1024]{3,2,1,0:T(8,128)(2,1)} %copy-done.1, bf16[4,4,128,1024]{3,2,1,0:T(8,128)(2,1)} %bitcast.22, bf16[2,128,1024]{2,1,0:T(8,128)(2,1)S(1)} %pad_maximum_fusion.na_ref, bf16[128,1024]{1,0:T(8,128)(2,1)S(1)} %collective-permute-done.3.nb_ref, ...), custom_call_target="tpu_custom_call" | custom-call | flops 3221225472 | bytes 11534336 | tf_op jit(solution)/shard_map/pallas_call | solution.py:124
  (4 shorter events, 0.0 us)
Async XLA Ops:
  0.0 1.0 copy-start
  0.0 107.6 %copy-start.2 = (s32[4096]{0:T(1024)S(1)}, s32[4096]{0:T(1024)}, u32[]{:S(2)}) copy-start(s32[4096]{0:T(1024)} %param.10) | copy-start | bytes 49156
  54.1 50.4 %collective-permute-start = (bf16[64,72,128]{2,1,0:T(8,128)(2,1)S(1)}, bf16[64,72,128]{2,1,0:T(8,128)(2,1)S(1)}, u32[]{:S(2)}, u32[]{:S(2)}) collective-permute-start(bf16[64,72,128]{2,1,0:T(8,128)(2,1)S(1)} %bitcast.18), channel_id=1, source_target_pairs={{0,4},{4,0},{1,5},{5,1},{2,6},{6,2},{3,7},{7,3},{8,12},{12,8},{9,1... | collective-permute-start | bytes 3538952 | tf_op jit(solution)/shard_map/ppermute | solution.py:23
  61.9 17.1 %collective-permute-start.3 = (bf16[128,1024]{1,0:T(8,128)(2,1)S(1)}, bf16[128,1024]{1,0:T(8,128)(2,1)S(1)}, u32[]{:S(2)}, u32[]{:S(2)}) collective-permute-start(bf16[128,1024]{1,0:T(8,128)(2,1)S(1)} %get-tuple-element.5), channel_id=1, source_target_pairs={{0,2},{1,3},{2,0},{3,1},{4,6},{5,7},{6,4},{7,5},{8,10},{9,11},{10,... | collective-permute-start | bytes 786440 | tf_op jit(solution)/shard_map/ppermute | solution.py:23
  65.7 25.9 %collective-permute-start.2 = (bf16[128,1024]{1,0:T(8,128)(2,1)}, bf16[128,1024]{1,0:T(8,128)(2,1)}, u32[]{:S(2)}, u32[]{:S(2)}) collective-permute-start(bf16[128,1024]{1,0:T(8,128)(2,1)} %get-tuple-element.6), channel_id=1, source_target_pairs={{0,3},{1,0},{2,1},{3,2},{4,7},{5,4},{6,5},{7,6},{8,11},{9,8},{10,9... | collective-permute-start | bytes 786440 | tf_op jit(solution)/shard_map/ppermute | solution.py:23
  69.6 22.0 %collective-permute-start.1 = (bf16[128,1024]{1,0:T(8,128)(2,1)S(1)}, bf16[128,1024]{1,0:T(8,128)(2,1)}, u32[]{:S(2)}, u32[]{:S(2)}) collective-permute-start(bf16[128,1024]{1,0:T(8,128)(2,1)S(1)} %get-tuple-element.7), channel_id=1, source_target_pairs={{0,1},{1,2},{2,3},{3,0},{4,5},{5,6},{6,7},{7,4},{8,9},{9,10},{10,1... | collective-permute-start | bytes 786440 | tf_op jit(solution)/shard_map/ppermute | solution.py:23
  79.0 23.3 %collective-permute-start.5 = (bf16[128,1024]{1,0:T(8,128)(2,1)S(1)}, bf16[128,1024]{1,0:T(8,128)(2,1)S(1)}, u32[]{:S(2)}, u32[]{:S(2)}) collective-permute-start(bf16[128,1024]{1,0:T(8,128)(2,1)S(1)} %collective-permute-done.3.nb_ref), channel_id=1, source_target_pairs={{0,128},{128,256},{256,384},{384,0},{1,129},{129,257},{257,385},{3... | collective-permute-start | bytes 786440 | tf_op jit(solution)/shard_map/ppermute | solution.py:23
  92.7 42.8 %collective-permute-start.4 = (bf16[2,128,1024]{2,1,0:T(8,128)(2,1)S(1)}, bf16[2,128,1024]{2,1,0:T(8,128)(2,1)S(1)}, u32[]{:S(2)}, u32[]{:S(2)}) collective-permute-start(bf16[2,128,1024]{2,1,0:T(8,128)(2,1)S(1)} %pad_maximum_fusion.na_ref), channel_id=1, source_target_pairs={{0,128},{128,256},{256,384},{384,0},{1,129},{129,257},{257,385},{3... | collective-permute-start | bytes 1572872 | tf_op jit(solution)/shard_map/ppermute | solution.py:23
  95.8 39.7 %collective-permute-start.6 = (bf16[2,128,1024]{2,1,0:T(8,128)(2,1)S(1)}, bf16[2,128,1024]{2,1,0:T(8,128)(2,1)S(1)}, u32[]{:S(2)}, u32[]{:S(2)}) collective-permute-start(bf16[2,128,1024]{2,1,0:T(8,128)(2,1)S(1)} %pad_maximum_fusion.na_ref), channel_id=1, source_target_pairs={{0,256},{128,384},{256,0},{384,128},{1,257},{129,385},{257,1},{385... | collective-permute-start | bytes 1572872 | tf_op jit(solution)/shard_map/ppermute | solution.py:23
  98.5 37.0 %collective-permute-start.8 = (bf16[2,128,1024]{2,1,0:T(8,128)(2,1)S(1)}, bf16[2,128,1024]{2,1,0:T(8,128)(2,1)S(1)}, u32[]{:S(2)}, u32[]{:S(2)}) collective-permute-start(bf16[2,128,1024]{2,1,0:T(8,128)(2,1)S(1)} %pad_maximum_fusion.na_ref), channel_id=1, source_target_pairs={{0,384},{128,0},{256,128},{384,256},{1,385},{129,1},{257,129},{385... | collective-permute-start | bytes 1572872 | tf_op jit(solution)/shard_map/ppermute | solution.py:23
  102.3 26.5 %collective-permute-start.7 = (bf16[128,1024]{1,0:T(8,128)(2,1)S(1)}, bf16[128,1024]{1,0:T(8,128)(2,1)S(1)}, u32[]{:S(2)}, u32[]{:S(2)}) collective-permute-start(bf16[128,1024]{1,0:T(8,128)(2,1)S(1)} %collective-permute-done.3.nb_ref), channel_id=1, source_target_pairs={{0,256},{128,384},{256,0},{384,128},{1,257},{129,385},{257,1},{385... | collective-permute-start | bytes 786440 | tf_op jit(solution)/shard_map/ppermute | solution.py:23
  104.6 31.0 %collective-permute-start.9 = (bf16[128,1024]{1,0:T(8,128)(2,1)S(1)}, bf16[128,1024]{1,0:T(8,128)(2,1)S(1)}, u32[]{:S(2)}, u32[]{:S(2)}) collective-permute-start(bf16[128,1024]{1,0:T(8,128)(2,1)S(1)} %collective-permute-done.3.nb_ref), channel_id=1, source_target_pairs={{0,384},{128,0},{256,128},{384,256},{1,385},{129,1},{257,129},{385... | collective-permute-start | bytes 786440 | tf_op jit(solution)/shard_map/ppermute | solution.py:23
  121.1 2.7 %copy-start.1 = (bf16[4,3,256,1024]{3,2,1,0:T(8,128)(2,1)}, bf16[4,3,256,1024]{3,2,1,0:T(8,128)(2,1)S(1)}, u32[]{:S(2)}) copy-start(bf16[4,3,256,1024]{3,2,1,0:T(8,128)(2,1)S(1)} %shard_map.64.s_ref) | copy-start | bytes 18874372

commit v2 on v1

v2 whole, which is shorter than its diff:
```python
import jax
import jax.numpy as jnp
from jax import lax
from jax.experimental import pallas as pl
from jax.experimental.pallas import tpu as pltpu
from jax.sharding import Mesh, PartitionSpec as P

P_SIZE = 1024
LANES = 128
TILE = 512
BLOCK = 256
WIDTH = 32
NT = (((1,), (1,)), ((), ()))
FREE = pl.CostEstimate(flops=1000, bytes_accessed=1000, transcendentals=0)
VM = pl.BlockSpec(memory_space=pltpu.VMEM)
SM = pl.BlockSpec(memory_space=pltpu.SMEM)
ANY = pl.BlockSpec(memory_space=pl.ANY)


def everyone(x, axes):
    n = lax.axis_size(axes)
    return lax.all_to_all(jnp.broadcast_to(x[None], (n,) + x.shape), axes, 0, 0)


def shifted(x, axis, by):
    n = lax.axis_size(axis)
    return lax.ppermute(x, axis, [(i, (i + by) % n) for i in range(n)])


def order_kernel(order_ref, src_ref, s_ref, lt_ref, mt_ref):
    width = 32

    @pl.when(pl.program_id(0) == 0)
    def _():
        for q in range(32):
            for a in range(2):
                blk = src_ref[4 * q:4 * q + 4, a * width:(a + 1) * width, :].reshape(LANES, LANES)
                lt_ref[a * LANES:(a + 1) * LANES, q * LANES:(q + 1) * LANES] = blk.T
        mt_ref[...] = src_ref[:, 2 * width, :].astype(jnp.float32).T.astype(jnp.bfloat16)

    e = order_ref[...]
    j = e & 31
    q = e >> 5
    d = ((q >> 2) & 1) * 64 + ((q >> 3) & 7) * 8 + (q >> 6) * 4 + (q & 3)
    storage = d * width + j
    acc = jnp.zeros((2 * LANES, TILE), jnp.float32)
    rows = lax.broadcasted_iota(jnp.int32, (BLOCK, TILE), 0)
    for b in range(4096 // BLOCK):
        hot = jnp.where(rows == storage - b * BLOCK, 1.0, 0.0).astype(jnp.bfloat16)
        acc += jnp.dot(lt_ref[:, b * BLOCK:(b + 1) * BLOCK], hot, preferred_element_type=jnp.float32)
    src_rows = lax.broadcasted_iota(jnp.int32, (LANES, TILE), 0)
    picked = jnp.dot(mt_ref[...], jnp.where(src_rows == d, 1.0, 0.0).astype(jnp.bfloat16), preferred_element_type=jnp.float32)
    at_j = lax.broadcasted_iota(jnp.int32, (width, TILE), 0) == j
    parts = [
        jnp.sum(jnp.where(at_j, picked[i * width:(i + 1) * width], 0.0), axis=0, keepdims=True) for i in range(4)
    ]
    w = parts[0] + parts[1]
    lam = parts[2] + parts[3]
    s_ref[0] = (acc * w).astype(jnp.bfloat16)
    s_ref[1] = (acc * (w * lam)).astype(jnp.bfloat16)
    s_ref[2] = (acc * (w * lam * lam)).astype(jnp.bfloat16)


def ordered_powers(pair_order, src):
    k = pair_order.shape[0]
    return pl.pallas_call(
        order_kernel,
        grid=(k // TILE,),
        in_specs=[
            pl.BlockSpec((1, TILE), lambda t: (0, t)),
            pl.BlockSpec(src.shape, lambda t: (0, 0, 0)),
        ],
        out_specs=pl.BlockSpec((3, 2 * LANES, TILE), lambda t: (0, 0, t)),
        out_shape=jax.ShapeDtypeStruct((3, 2 * LANES, k), jnp.bfloat16),
        scratch_shapes=[pltpu.VMEM((2 * LANES, k), jnp.bfloat16), pltpu.VMEM((LANES, LANES), jnp.bfloat16)],
        compiler_params=pltpu.CompilerParams(vmem_limit_bytes=32 * 2**20),
        cost_estimate=pl.CostEstimate(flops=2 * k * k * 256, bytes_accessed=12 * 2**20, transcendentals=0),
    )(pair_order[None], src)


def lanes(d, n, group):
    return pl.ds(pl.multiple_of(((d + n) % 4) * group, LANES), group)


def own_kernel(at_ref, s_ref, rv_ref, o_ref, rhs_ref, sem):
    d = at_ref[1]
    copy = pltpu.make_async_copy(rv_ref.at[d], rhs_ref, sem)
    copy.start()
    copy.wait()
    for m in range(3):
        for c in range(2):
            cols = slice(c * 256, (c + 1) * 256)
            o_ref[m, :, cols] = lax.dot_general(
                s_ref[m, :, lanes(d, 0, rhs_ref.shape[1])], rhs_ref[cols, :], NT, preferred_element_type=jnp.float32
            )


def contract_kernel(at_ref, s_ref, acc_ref, p0, p1, p2, p3, o_ref, rhs_ref, sum_ref, sem):
    r, d = at_ref[0], at_ref[1]
    step = p0.shape[1]
    group = rhs_ref.shape[2]
    copies = []
    for n in (1, 2, 3):
        srcs = (p0.at[(d + n) % 4], p1.at[n - 1], p2.at[(d + n) % 4], p3.at[n - 1])
        at_n = []
        for t, src in enumerate(srcs):
            rows = pl.ds(pl.multiple_of(((r - t + 4) % 4) * step, 128), step)
            at_n.append(pltpu.make_async_copy(src, rhs_ref.at[n - 1, rows], sem.at[4 * n - 4 + t]))
        copies.append(at_n)
    for at_n in copies:
        for copy in at_n:
            copy.start()
    for n in (1, 2, 3):
        for copy in copies[n - 1]:
            copy.wait()
        for c in range(2):
            cols = slice(c * 256, (c + 1) * 256)
            for m in range(3):
                acc = lax.dot_general(
                    s_ref[m, :, lanes(d, n, group)], rhs_ref[n - 1, cols, :], NT, preferred_element_type=jnp.float32
                )
                acc += acc_ref[m, :, cols] if n == 1 else sum_ref[m, :, cols]
                if n < 3:
                    sum_ref[m, :, cols] = acc
                else:
                    o_ref[m, :, cols] = acc.astype(jnp.bfloat16)


def contract(at, s, rv, parts):
    _, block, group = rv.shape
    summed = pl.pallas_call(
        own_kernel,
        in_specs=[SM, VM, ANY],
        out_specs=VM,
        out_shape=jax.ShapeDtypeStruct((3, 2 * LANES, block), jnp.float32),
        scratch_shapes=[pltpu.VMEM((block, group), jnp.bfloat16), pltpu.SemaphoreType.DMA(())],
        compiler_params=pltpu.CompilerParams(vmem_limit_bytes=24 * 2**20),
        cost_estimate=FREE,
    )(at, s, rv)
    return pl.pallas_call(
        contract_kernel,
        in_specs=[SM, VM, VM] + [ANY] * len(parts),
        out_specs=VM,
        out_shape=jax.ShapeDtypeStruct((3, 2 * LANES, block), jnp.bfloat16),
        scratch_shapes=[
            pltpu.VMEM((3, block, group), jnp.bfloat16),
            pltpu.VMEM((3, 2 * LANES, block), jnp.float32),
            pltpu.SemaphoreType.DMA((12,)),
        ],
        compiler_params=pltpu.CompilerParams(vmem_limit_bytes=24 * 2**20),
        cost_estimate=FREE,
    )(at, s, summed, *parts)


def split(v):
    hi = lax.reduce_precision(v, 8, 7)
    return [hi.astype(jnp.bfloat16), (v - hi).astype(jnp.bfloat16)]


def on_device(left_slab, right_vectors, pair_weight, eigenvalue, pair_order, row_offset):
    n_depth, n_row = lax.axis_size("depth"), lax.axis_size("row")
    r, d = lax.axis_index("row"), lax.axis_index("depth")
    at = jnp.stack([r, d])
    panel_rows = P_SIZE // n_row
    cols, group = right_vectors.shape
    block = cols // n_depth
    quarter = block // n_row

    start = row_offset[0] + r * panel_rows
    mine = lax.dynamic_slice_in_dim(left_slab.T, start, panel_rows, 1)
    scal = jnp.concatenate(split(pair_weight) + split(eigenvalue))
    scal = jnp.broadcast_to(scal[None], (8, LANES))
    mine = jnp.concatenate([mine[:, :LANES], mine[:, LANES:], scal], axis=0)
    by_z = everyone(mine, ("zlo", "depth"))
    both = lax.all_gather(by_z, ("core", "y"), axis=0, tiled=True)

    rv = right_vectors.reshape(n_depth, block, group)
    first = lax.dynamic_slice_in_dim(rv, r * quarter, quarter, 1)
    first, _ = lax.optimization_barrier((first, by_z))
    first = lax.all_to_all(first, "depth", 0, 0)
    others = jnp.concatenate([lax.dynamic_index_in_dim(first, (d + n) % n_depth, 0) for n in (1, 2, 3)])
    second = lax.dynamic_slice_in_dim(rv, ((r + 2) % n_row) * quarter, quarter, 1)
    second, _ = lax.optimization_barrier((second, others))
    second = lax.all_to_all(second, "depth", 0, 0)
    parts = [first, shifted(others, "row", 1), second, shifted(others, "row", 3)]

    both, _ = lax.optimization_barrier((both, others))
    s = ordered_powers(pair_order, both)
    return contract(at, s, rv, parts)


def solution(mesh):
    fine = Mesh(mesh.devices.reshape(4, 2, 8, 2, 4), ("row", "zlo", "y", "core", "depth"))
    col = ("zlo", "y", "core")
    all_k = col + ("depth",)
    in_specs = (P(None, all_k), P(col, "depth"), P(all_k), P(all_k), P(), P())
    return jax.shard_map(on_device, mesh=fine, in_specs=in_specs, out_specs=P(None, "row", all_k), check_vma=False)
```

time: 144 us -> 107 us (0.74)
  the two profiles are of different devices: /device:TPU:3 before, /device:TPU:80 now
where the time goes in v2:
time: 107 us; the launch traced here: 106 us
  waiting for transfers between devices  28.8 us (27%)
  Pallas kernels  20.4 us (19%)
  blocking collectives  17.7 us (17%)
  starting transfers between devices  14.5 us (14%)
  between operations  14.3 us (13%)
  local copies, waits for them, and re-layouts  8.93 us (8%)
  other arithmetic  1.81 us (2%)
    all_to_all x1, waiting for transfers between devices, on_device(): first = lax.all_to_all(first, 'depth', 0, 0)  26.6 us
    all_to_all x1, blocking collectives, everyone(): return lax.all_to_all(jnp.broadcast_to(x[None], (n,) + x.shape), axes, 0, 0)  17.7 us
    pallas_call x1, Pallas kernels, ordered_powers(): pl.pallas_call(order_kernel, grid=(k // TILE,), in_specs=[pl.BlockSpec((1...  13.2 us
    ppermute x2, starting transfers between devices, shifted(): return lax.ppermute(x, axis, [(i, (i + by) % n) for i in range(n)])  6.58 us
    unnamed x12, local copies, waits for them, and re-layouts  5.72 us
    pallas_call x1, Pallas kernels, contract(): pl.pallas_call(contract_kernel, in_specs=[SM, VM, VM] + [ANY] * len(parts...  5.62 us
    all_to_all x1, starting transfers between devices, on_device(): second = lax.all_to_all(second, 'depth', 0, 0)  4.24 us
    all_to_all x1, starting transfers between devices, on_device(): first = lax.all_to_all(first, 'depth', 0, 0)  3.65 us
  transfers between devices with their start and end apart: 5, of which 2 were waited for; matrix products, arithmetic and copies ran while one was open for 4% of the time, Pallas kernels for 14%

profile of v2, /device:TPU:80, one launch (start us, length us, event | category | flops | bytes accessed | tf_op | source)
XLA Modules:
  0.0 106.3 jit_solution(11622877800965063769)
XLA Ops:
  6.5 0.0 copy-start
  6.5 0.0 all-gather.2.cloned.1.call-start
  7.2 0.3 copy-done
  7.5 0.1 dynamic-slice_bitcast_fusion
  7.6 0.7 reduce-precision_convert_fusion
  8.3 0.1 pad_maximum_fusion.2
  8.4 17.7 %all_to_all.15 = bf16[8,72,128]{2,1,0:T(8,128)(2,1)} all-to-all(bf16[8,72,128]{2,1,0:T(8,128)(2,1)S(1)} %broadcast_in_dim.8), channel_id=1, replica_groups=mesh['row'=4,'zlo'=2,'y'=8,'core'=2,'depth'=4] {'zlo','depth'}, dimensions={0} | all-to-all | bytes 294912 | tf_op jit(solution)/shard_map/all_to_all | solution.py:22
  26.0 0.0 all-gather.2.cloned.1.call-update
  26.1 3.0 %constant_dynamic-slice_fusion = (bf16[4,128,1024]{2,1,0:T(8,128)(2,1)}, bf16[4,128,1024]{2,1,0:T(8,128)(2,1)}) fusion(bf16[4,512,1024]{2,1,0:T(8,128)(2,1)} %bitcast.8, s32[]{:T(128)S(6)} %select_n.47, s32[]{:T(128)S(6)} %select_n.39), kind=kLoop, calls=%fused_computation.3 | loop fusion | bytes 4194312 | tf_op jit(solution)/shard_map/dynamic_slice | solution.py:182
  29.1 0.0 copy-start.5
  29.1 3.6 %all-to-all-start.1 = ((bf16[4,128,1024]{2,1,0:T(8,128)(2,1)}), bf16[4,128,1024]{2,1,0:T(8,128)(2,1)S(1)}, u32[]{:S(2)}, u32[]{:S(2)}) async-start(bf16[4,128,1024]{2,1,0:T(8,128)(2,1)} %get-tuple-element.8), calls=%async_computation.1 | async-start | bytes 2097152 | tf_op jit(solution)/shard_map/all_to_all | solution.py:180
  32.8 26.6 %all-to-all-done.1.p0 = bf16[4,128,1024]{2,1,0:T(8,128)(2,1)S(1)} async-done(((bf16[4,128,1024]{2,1,0:T(8,128)(2,1)}), bf16[4,128,1024]{2,1,0:T(8,128)(2,1)S(1)}, u32[]{:S(2)}, u32[]{:S(2)}) %all-to-all-start.1) | async-done | bytes 1048608 | tf_op jit(solution)/shard_map/all_to_all | solution.py:180
  59.4 0.1 constant_dynamic-slice_fusion.3
  59.5 1.0 pad_maximum_fusion
  60.5 4.2 %all-to-all-start.2 = ((bf16[4,128,1024]{2,1,0:T(8,128)(2,1)}), bf16[4,128,1024]{2,1,0:T(8,128)(2,1)}, u32[]{:S(2)}, u32[]{:S(2)}) async-start(bf16[4,128,1024]{2,1,0:T(8,128)(2,1)} %get-tuple-element.10), calls=%async_computation.2 | async-start | bytes 2097152 | tf_op jit(solution)/shard_map/all_to_all | solution.py:184
  64.7 0.1 pad_add_fusion.at_ref
  64.8 4.7 %collective-permute-start.1 = (bf16[3,128,1024]{2,1,0:T(8,128)(2,1)}, bf16[3,128,1024]{2,1,0:T(8,128)(2,1)}, u32[]{:S(2)}, u32[]{:S(2)}) collective-permute-start(bf16[3,128,1024]{2,1,0:T(8,128)(2,1)} %pad_maximum_fusion), channel_id=1, source_target_pairs={{0,384},{128,0},{256,128},{384,256},{1,385},{129,1},{257,129},{385... | collective-permute-start | bytes 2359304 | tf_op jit(solution)/shard_map/ppermute | solution.py:27
  69.4 1.9 %collective-permute-start = (bf16[3,128,1024]{2,1,0:T(8,128)(2,1)}, bf16[3,128,1024]{2,1,0:T(8,128)(2,1)}, u32[]{:S(2)}, u32[]{:S(2)}) collective-permute-start(bf16[3,128,1024]{2,1,0:T(8,128)(2,1)} %pad_maximum_fusion), channel_id=1, source_target_pairs={{0,128},{128,256},{256,384},{384,0},{1,129},{129,257},{257,385},{3... | collective-permute-start | bytes 2359304 | tf_op jit(solution)/shard_map/ppermute | solution.py:27
  71.4 0.0 all-gather.2.cloned.1.call-done.src_ref
  71.4 0.0 copy-done.5
  71.4 0.0 copy-start.4
  71.4 1.7 %copy-done.4 = bf16[128,72,128]{2,1,0:T(8,128)(2,1)S(1)} copy-done((bf16[128,72,128]{2,1,0:T(8,128)(2,1)S(1)}, bf16[128,72,128]{2,1,0:T(8,128)(2,1)}, u32[]{:S(2)}) %copy-start.4) | copy-done | bytes 2359320
  73.1 0.0 copy-start.3
  73.1 13.2 %shard_map.64.s_ref = bf16[3,256,4096]{2,1,0:T(8,128)(2,1)S(1)} custom-call(s32[1,4096]{1,0:T(1,128)S(1)} %bitcast.10, bf16[128,72,128]{2,1,0:T(8,128)(2,1)S(1)} %copy-done.4), custom_call_target="tpu_custom_call" | custom-call | flops 8589934592 | bytes 12582912 | tf_op jit(solution)/shard_map/pallas_call | solution.py:66
  86.2 0.0 copy-done.3
  86.3 0.0 copy-start.1
  86.3 1.6 %shard_map.65.acc_ref = f32[3,256,512]{2,1,0:T(8,128)S(1)} custom-call(s32[2]{0:T(128)S(1)} %pad_add_fusion.at_ref, bf16[3,256,4096]{2,1,0:T(8,128)(2,1)S(1)} %shard_map.64.s_ref, bf16[4,512,1024]{2,1,0:T(8,128)(2,1)S(1)} %bitcast.9), custom_call_target="tpu_custom_call" | custom-call | flops 1000 | bytes 1000 | tf_op jit(solution)/shard_map/pallas_call | solution.py:131
  87.9 1.0 copy-done.1
  88.9 0.0 collective-permute-done.1.p3
  88.9 2.1 %collective-permute-done.p1 = bf16[3,128,1024]{2,1,0:T(8,128)(2,1)} collective-permute-done((bf16[3,128,1024]{2,1,0:T(8,128)(2,1)}, bf16[3,128,1024]{2,1,0:T(8,128)(2,1)}, u32[]{:S(2)}, u32[]{:S(2)}) %collective-permute-start) | collective-permute-done | bytes 786464 | tf_op jit(solution)/shard_map/ppermute | solution.py:27
  91.0 0.0 all-to-all-done.2.p2
  91.0 0.0 copy-start.2
  91.0 2.8 %copy-done.2 = bf16[3,256,4096]{2,1,0:T(8,128)(2,1)S(1)} copy-done((bf16[3,256,4096]{2,1,0:T(8,128)(2,1)S(1)}, bf16[3,256,4096]{2,1,0:T(8,128)(2,1)}, u32[]{:S(2)}) %copy-start.2) | copy-done | bytes 6291480
  93.8 5.6 %shard_map.66 = bf16[3,256,512]{2,1,0:T(8,128)(2,1)} custom-call(s32[2]{0:T(128)S(1)} %pad_add_fusion.at_ref, bf16[3,256,4096]{2,1,0:T(8,128)(2,1)S(1)} %copy-done.2, f32[3,256,512]{2,1,0:T(8,128)S(1)} %shard_map.65.acc_ref, bf16[4,128,1024]{2,1,0:T(8,128)(2,1)S(1)} %all-to-all-done.1.p0, bf16[3,128,1024]{2,1,0:T(8,128)(2,1)} %collective-permute-done.p1, ...), custom_call_target="tpu_custom_call" | custom-call | flops 1000 | bytes 1000 | tf_op jit(solution)/shard_map/pallas_call | solution.py:140
  (4 shorter events, 0.0 us)
Async XLA Ops:
  6.5 1.0 copy-start
  6.5 64.9 %all-gather.2.cloned.1.call-start = ((), (), s32[]{:S(2)}) async-start(), calls=%async_computation.3 | async-start | bytes 2506752 | tf_op jit(solution)/shard_map/all_gather | solution.py:175
  29.1 42.3 %copy-start.5 = (s32[4096]{0:T(1024)S(1)}, s32[4096]{0:T(1024)}, u32[]{:S(2)}) copy-start(s32[4096]{0:T(1024)} %param.10) | copy-start | bytes 49156
  29.1 30.3 %all-to-all-start.1 = ((bf16[4,128,1024]{2,1,0:T(8,128)(2,1)}), bf16[4,128,1024]{2,1,0:T(8,128)(2,1)S(1)}, u32[]{:S(2)}, u32[]{:S(2)}) async-start(bf16[4,128,1024]{2,1,0:T(8,128)(2,1)} %get-tuple-element.8), calls=%async_computation.1 | async-start | bytes 2097152 | tf_op jit(solution)/shard_map/all_to_all | solution.py:180
  60.5 30.6 %all-to-all-start.2 = ((bf16[4,128,1024]{2,1,0:T(8,128)(2,1)}), bf16[4,128,1024]{2,1,0:T(8,128)(2,1)}, u32[]{:S(2)}, u32[]{:S(2)}) async-start(bf16[4,128,1024]{2,1,0:T(8,128)(2,1)} %get-tuple-element.10), calls=%async_computation.2 | async-start | bytes 2097152 | tf_op jit(solution)/shard_map/all_to_all | solution.py:184
  64.8 24.1 %collective-permute-start.1 = (bf16[3,128,1024]{2,1,0:T(8,128)(2,1)}, bf16[3,128,1024]{2,1,0:T(8,128)(2,1)}, u32[]{:S(2)}, u32[]{:S(2)}) collective-permute-start(bf16[3,128,1024]{2,1,0:T(8,128)(2,1)} %pad_maximum_fusion), channel_id=1, source_target_pairs={{0,384},{128,0},{256,128},{384,256},{1,385},{129,1},{257,129},{385... | collective-permute-start | bytes 2359304 | tf_op jit(solution)/shard_map/ppermute | solution.py:27
  69.4 21.6 %collective-permute-start = (bf16[3,128,1024]{2,1,0:T(8,128)(2,1)}, bf16[3,128,1024]{2,1,0:T(8,128)(2,1)}, u32[]{:S(2)}, u32[]{:S(2)}) collective-permute-start(bf16[3,128,1024]{2,1,0:T(8,128)(2,1)} %pad_maximum_fusion), channel_id=1, source_target_pairs={{0,128},{128,256},{256,384},{384,0},{1,129},{129,257},{257,385},{3... | collective-permute-start | bytes 2359304 | tf_op jit(solution)/shard_map/ppermute | solution.py:27
  71.4 1.7 %copy-start.4 = (bf16[128,72,128]{2,1,0:T(8,128)(2,1)S(1)}, bf16[128,72,128]{2,1,0:T(8,128)(2,1)}, u32[]{:S(2)}) copy-start(bf16[128,72,128]{2,1,0:T(8,128)(2,1)} %all-gather.2.cloned.1.call-done.src_ref) | copy-start | bytes 7077892
  73.1 13.2 %copy-start.3 = (bf16[2048,1024]{1,0:T(8,128)(2,1)S(1)}, bf16[2048,1024]{1,0:T(8,128)(2,1)}, u32[]{:S(2)}) copy-start(bf16[2048,1024]{1,0:T(8,128)(2,1)} %param.7) | copy-start | bytes 12582916
  86.3 2.7 %copy-start.1 = (bf16[3,256,4096]{2,1,0:T(8,128)(2,1)}, bf16[3,256,4096]{2,1,0:T(8,128)(2,1)S(1)}, u32[]{:S(2)}) copy-start(bf16[3,256,4096]{2,1,0:T(8,128)(2,1)S(1)} %shard_map.64.s_ref) | copy-start | bytes 18874372
  91.0 2.8 %copy-start.2 = (bf16[3,256,4096]{2,1,0:T(8,128)(2,1)S(1)}, bf16[3,256,4096]{2,1,0:T(8,128)(2,1)}, u32[]{:S(2)}) copy-start(bf16[3,256,4096]{2,1,0:T(8,128)(2,1)} %copy-done.1) | copy-start | bytes 18874372
Sparse Core Ops, SparseCore 0:
  26.2 38.2 all-gather.1

commit v3 on v2

v3 whole, which is shorter than its diff:
```python
import jax
import jax.numpy as jnp
from jax import lax
from jax.experimental import pallas as pl
from jax.experimental.pallas import tpu as pltpu
from jax.sharding import Mesh, PartitionSpec as P

P_SIZE = 1024
LANES = 128
TILE = 1024
BLOCK = 256
WIDTH = 32
NT = (((1,), (1,)), ((), ()))
FREE = pl.CostEstimate(flops=1000, bytes_accessed=1000, transcendentals=0)
VM = pl.BlockSpec(memory_space=pltpu.VMEM)
SM = pl.BlockSpec(memory_space=pltpu.SMEM)
ANY = pl.BlockSpec(memory_space=pl.ANY)
HBM = pl.BlockSpec(memory_space=pltpu.HBM)


def everyone(x, axes):
    n = lax.axis_size(axes)
    return lax.all_to_all(jnp.broadcast_to(x[None], (n,) + x.shape), axes, 0, 0)


def shifted(x, axis, by):
    n = lax.axis_size(axis)
    return lax.ppermute(x, axis, [(i, (i + by) % n) for i in range(n)])


def order_kernel(at_ref, order_ref, own_ref, other_ref, rv_ref, s_out, acc_out, lt_ref, mt_ref, rhs_ref, s_buf, acc_ref, sem, out_sem):
    t = pl.program_id(0)
    last = pl.num_programs(0) - 1
    steps = rhs_ref.shape[1] // TILE
    copy = pltpu.make_async_copy(rv_ref.at[at_ref[1]], rhs_ref, sem)
    acc_copy = pltpu.make_async_copy(acc_ref, acc_out, out_sem.at[2])
    slot = t % 2
    s_ref = s_buf.at[slot]

    def s_copy(step, at):
        ks = pl.ds(pl.multiple_of(step * TILE, TILE), TILE)
        return pltpu.make_async_copy(s_buf.at[at], s_out.at[:, :, ks], out_sem.at[at])

    @pl.when(t == 0)
    def _():
        copy.start()
        for h, src in enumerate((own_ref, other_ref)):
            for q in range(16):
                for a in range(2):
                    blk = src[4 * q:4 * q + 4, a * WIDTH:(a + 1) * WIDTH, :].reshape(LANES, LANES)
                    at = (16 * h + q) * LANES
                    lt_ref[a * LANES:(a + 1) * LANES, at:at + LANES] = blk.T
        mt = jnp.concatenate([own_ref[:, 2 * WIDTH, :], other_ref[:, 2 * WIDTH, :]], axis=0)
        mt_ref[...] = mt.astype(jnp.float32).T.astype(jnp.bfloat16)

    e = order_ref[...]
    j = e & 31
    q = e >> 5
    d = (((q >> 2) & 1) ^ at_ref[2]) * 64 + ((q >> 3) & 7) * 8 + (q >> 6) * 4 + (q & 3)
    storage = d * WIDTH + j
    acc = jnp.zeros((2 * LANES, TILE), jnp.float32)
    rows = lax.broadcasted_iota(jnp.int32, (BLOCK, TILE), 0)
    for b in range(4096 // BLOCK):
        hot = jnp.where(rows == storage - b * BLOCK, 1.0, 0.0).astype(jnp.bfloat16)
        acc += jnp.dot(lt_ref[:, b * BLOCK:(b + 1) * BLOCK], hot, preferred_element_type=jnp.float32)
    src_rows = lax.broadcasted_iota(jnp.int32, (LANES, TILE), 0)
    hot = jnp.where(src_rows == d, 1.0, 0.0).astype(jnp.bfloat16)
    picked = jnp.dot(mt_ref[...], hot, preferred_element_type=jnp.float32)
    at_j = lax.broadcasted_iota(jnp.int32, (WIDTH, TILE), 0) == j
    parts = [jnp.sum(jnp.where(at_j, picked[i * WIDTH:(i + 1) * WIDTH], 0.0), axis=0, keepdims=True) for i in range(4)]
    w = parts[0] + parts[1]
    lam = parts[2] + parts[3]

    @pl.when(t >= 2)
    def _():
        s_copy(t - 2, slot).wait()

    s_ref[0] = (acc * w).astype(jnp.bfloat16)
    s_ref[1] = (acc * (w * lam)).astype(jnp.bfloat16)
    s_ref[2] = (acc * (w * lam * lam)).astype(jnp.bfloat16)

    s_copy(t, slot).start()

    @pl.when(t == at_ref[1] * steps)
    def _():
        copy.wait()
        acc_ref[...] = jnp.zeros_like(acc_ref)

    @pl.when(t // steps == at_ref[1])
    def _():
        ks = pl.ds(pl.multiple_of((t % steps) * TILE, TILE), TILE)
        for m in range(3):
            for c in range(2):
                cols = slice(c * 256, (c + 1) * 256)
                acc_ref[m, :, cols] += lax.dot_general(
                    s_ref[m], rhs_ref[cols, ks], NT, preferred_element_type=jnp.float32
                )

    @pl.when(t == (at_ref[1] + 1) * steps - 1)
    def _():
        acc_copy.start()

    @pl.when(t == last)
    def _():
        s_copy(t - 1, 1 - slot).wait()
        s_copy(t, slot).wait()
        acc_copy.wait()


def ordered_powers(at, pair_order, own, other, rv):
    k = pair_order.shape[0]
    _, block, group = rv.shape
    whole = pl.BlockSpec(own.shape, lambda t: (0, 0, 0))
    return pl.pallas_call(
        order_kernel,
        grid=(k // TILE,),
        in_specs=[SM, pl.BlockSpec((1, TILE), lambda t: (0, t)), whole, whole, ANY],
        out_specs=[HBM, HBM],
        out_shape=[
            pltpu.HBM((3, 2 * LANES, k), jnp.bfloat16),
            pltpu.HBM((3, 2 * LANES, block), jnp.float32),
        ],
        scratch_shapes=[
            pltpu.VMEM((2 * LANES, k), jnp.bfloat16),
            pltpu.VMEM((LANES, LANES), jnp.bfloat16),
            pltpu.VMEM((block, group), jnp.bfloat16),
            pltpu.VMEM((2, 3, 2 * LANES, TILE), jnp.bfloat16),
            pltpu.VMEM((3, 2 * LANES, block), jnp.float32),
            pltpu.SemaphoreType.DMA(()),
            pltpu.SemaphoreType.DMA((3,)),
        ],
        compiler_params=pltpu.CompilerParams(vmem_limit_bytes=24 * 2**20),
        cost_estimate=FREE,
    )(at, pair_order[None], own, other, pltpu.with_memory_space_constraint(rv, pltpu.HBM))


def lanes(d, n, group):
    return pl.ds(pl.multiple_of(((d + n) % 4) * group, LANES), group)


def contract_kernel(at_ref, s_ref, acc_ref, p0, p1, p2, p3, o_ref, rhs_ref, sum_ref, s_buf, sem):
    r, d = at_ref[0], at_ref[1]
    step = p0.shape[1]
    group = rhs_ref.shape[2]
    copies = []
    for n in (1, 2, 3):
        at_n = [pltpu.make_async_copy(s_ref.at[:, :, lanes(d, n, group)], s_buf.at[n - 1], sem.at[5 * n - 5])]
        for t, src in enumerate((p0.at[n - 1], p1.at[n - 1], p2.at[(d + n) % 4], p3.at[n - 1])):
            rows = pl.ds(pl.multiple_of(((r - t + 4) % 4) * step, LANES), step)
            at_n.append(pltpu.make_async_copy(src, rhs_ref.at[n - 1, rows], sem.at[5 * n - 4 + t]))
        copies.append(at_n)
    copies[0].append(pltpu.make_async_copy(acc_ref, sum_ref, sem.at[15]))
    for at_n in copies:
        for copy in at_n:
            copy.start()
    for n in (1, 2, 3):
        for copy in copies[n - 1]:
            copy.wait()
        for c in range(2):
            cols = slice(c * 256, (c + 1) * 256)
            for m in range(3):
                acc = sum_ref[m, :, cols] + lax.dot_general(
                    s_buf[n - 1, m], rhs_ref[n - 1, cols, :], NT, preferred_element_type=jnp.float32
                )
                if n < 3:
                    sum_ref[m, :, cols] = acc
                else:
                    o_ref[m, :, cols] = acc.astype(jnp.bfloat16)


def contract(at, s, summed, parts):
    group, block = parts[0].shape[2], 4 * parts[0].shape[1]
    return pl.pallas_call(
        contract_kernel,
        in_specs=[SM, HBM, HBM] + [ANY] * len(parts),
        out_specs=VM,
        out_shape=jax.ShapeDtypeStruct((3, 2 * LANES, block), jnp.bfloat16),
        scratch_shapes=[
            pltpu.VMEM((3, block, group), jnp.bfloat16),
            pltpu.VMEM((3, 2 * LANES, block), jnp.float32),
            pltpu.VMEM((3, 3, 2 * LANES, group), jnp.bfloat16),
            pltpu.SemaphoreType.DMA((16,)),
        ],
        compiler_params=pltpu.CompilerParams(vmem_limit_bytes=20 * 2**20),
        cost_estimate=FREE,
    )(at, *(pltpu.with_memory_space_constraint(v, pltpu.HBM) for v in (s, summed)), *parts)


def split(v):
    hi = lax.reduce_precision(v, 8, 7)
    return [hi.astype(jnp.bfloat16), (v - hi).astype(jnp.bfloat16)]


def on_device(left_slab, right_vectors, pair_weight, eigenvalue, pair_order, row_offset):
    n_depth, n_row = lax.axis_size("depth"), lax.axis_size("row")
    r, d = lax.axis_index("row"), lax.axis_index("depth")
    at = jnp.stack([r, d, lax.axis_index("core")])
    panel_rows = P_SIZE // n_row
    cols, group = right_vectors.shape
    block = cols // n_depth
    quarter = block // n_row

    start = row_offset[0] + r * panel_rows
    mine = lax.dynamic_slice_in_dim(left_slab.T, start, panel_rows, 1)
    scal = jnp.concatenate(split(pair_weight) + split(eigenvalue))
    scal = jnp.broadcast_to(scal[None], (8, LANES))
    mine = jnp.concatenate([mine[:, :LANES], mine[:, LANES:], scal], axis=0)
    by_z = everyone(mine, ("zlo", "depth"))
    same = everyone(by_z, "y").reshape(64, 72, LANES)

    rv = right_vectors.reshape(n_depth, block, group)

    def first(n):
        piece = lax.dynamic_slice(rv, ((d - n) % n_depth, r * quarter, 0), (1, quarter, group))
        return shifted(piece, "depth", n_depth - n)

    others = jnp.concatenate([first(n) for n in (1, 2, 3)])
    same, others = lax.optimization_barrier((same, others))
    rv_later, _ = lax.optimization_barrier((rv, by_z))
    second = lax.dynamic_slice_in_dim(rv_later, ((r + 2) % n_row) * quarter, quarter, 1)
    second, _ = lax.optimization_barrier((second, others))
    second = lax.all_to_all(second, "depth", 0, 0)
    parts = [others, shifted(others, "row", 1), second, shifted(others, "row", 3)]

    other = shifted(same, "core", 1)
    s, summed = ordered_powers(at, pair_order, same, other, rv)
    return contract(at, s, summed, parts)


def solution(mesh):
    fine = Mesh(mesh.devices.reshape(4, 2, 8, 2, 4), ("row", "zlo", "y", "core", "depth"))
    col = ("zlo", "y", "core")
    all_k = col + ("depth",)
    in_specs = (P(None, all_k), P(col, "depth"), P(all_k), P(all_k), P(), P())
    return jax.shard_map(on_device, mesh=fine, in_specs=in_specs, out_specs=P(None, "row", all_k), check_vma=False)
```

time: 107 us -> 98.2 us (0.918)
  the two profiles are of different devices: /device:TPU:80 before, /device:TPU:78 now
where the time goes in v3:
time: 98.2 us; the launch traced here: 97.6 us
  starting transfers between devices  29.1 us (30%)
  waiting for transfers between devices  22.7 us (23%)
  Pallas kernels  21.6 us (22%)
  blocking collectives  17.6 us (18%)
  local copies, waits for them, and re-layouts  5 us (5%)
    ppermute x6, waiting for transfers between devices, shifted(): return lax.ppermute(x, axis, [(i, (i + by) % n) for i in range(n)])  22.7 us
    ppermute x6, starting transfers between devices, shifted(): return lax.ppermute(x, axis, [(i, (i + by) % n) for i in range(n)])  18 us
    all_to_all x1, blocking collectives, everyone(): return lax.all_to_all(jnp.broadcast_to(x[None], (n,) + x.shape), axes, 0, 0)  17.6 us
    pallas_call x1, Pallas kernels, ordered_powers(): pl.pallas_call(order_kernel, grid=(k // TILE,), in_specs=[SM, pl.BlockSpe...  15 us
    all_to_all x1, starting transfers between devices, everyone(): return lax.all_to_all(jnp.broadcast_to(x[None], (n,) + x.shape), axes, 0, 0)  7.55 us
    pallas_call x1, Pallas kernels, contract(): pl.pallas_call(contract_kernel, in_specs=[SM, HBM, HBM] + [ANY] * len(par...  6.6 us
    all_to_all x1, starting transfers between devices, on_device(): second = lax.all_to_all(second, 'depth', 0, 0)  3.53 us
    dynamic_slice x1, local copies, waits for them, and re-layouts, on_device(): lax.dynamic_slice_in_dim(rv_later, (r + 2) % n_row * quarter, quarter, 1)  2.26 us
  transfers between devices with their start and end apart: 8, of which 5 were waited for; matrix products, arithmetic and copies ran while one was open for 4% of the time, Pallas kernels for 15%

profile of v3, /device:TPU:78, one launch (start us, length us, event | category | flops | bytes accessed | tf_op | source)
XLA Modules:
  0.0 97.6 jit_solution(4912102636449420664)
XLA Ops:
  0.0 0.0 copy-start
  0.7 0.3 copy-done
  1.0 0.1 dynamic-slice_bitcast_fusion
  1.1 0.7 reduce-precision_convert_fusion
  1.7 0.1 pad_maximum_fusion.2
  1.9 17.6 %all_to_all.15 = bf16[8,72,128]{2,1,0:T(8,128)(2,1)S(1)} all-to-all(bf16[8,72,128]{2,1,0:T(8,128)(2,1)S(1)} %broadcast_in_dim.10), channel_id=1, replica_groups=mesh['row'=4,'zlo'=2,'y'=8,'core'=2,'depth'=4] {'zlo','depth'}, dimensions={0} | all-to-all | bytes 294912 | tf_op jit(solution)/shard_map/all_to_all | solution.py:23
  19.4 1.2 %broadcast_in_dim.11 = bf16[8,8,72,128]{3,2,1,0:T(8,128)(2,1)} broadcast(bf16[8,72,128]{2,1,0:T(8,128)(2,1)S(1)} %all_to_all.15), dimensions={1,2,3} | broadcast | bytes 1327104 | tf_op jit(solution)/shard_map/broadcast_in_dim | solution.py:23
  20.6 7.5 %all-to-all-start.1 = ((bf16[8,8,72,128]{3,2,1,0:T(8,128)(2,1)}), bf16[8,8,72,128]{3,2,1,0:T(8,128)(2,1)S(1)}, u32[]{:S(2)}, u32[]{:S(2)}) async-start(bf16[8,8,72,128]{3,2,1,0:T(8,128)(2,1)} %broadcast_in_dim.11), calls=%async_computation.1 | async-start | bytes 2359296 | tf_op jit(solution)/shard_map/all_to_all | solution.py:23
  28.1 0.0 copy-start.1
  28.1 1.2 %constant_dynamic-slice_fusion.3 = (bf16[1,128,1024]{2,1,0:T(8,128)(2,1)S(1)}, bf16[1,128,1024]{2,1,0:T(8,128)(2,1)S(1)}, bf16[1,128,1024]{2,1,0:T(8,128)(2,1)S(1)}) fusion(bf16[4,512,1024]{2,1,0:T(8,128)(2,1)} %bitcast.13, s32[]{:T(128)S(6)} %select_n.41, s32[]{:T(128)S(6)} %select_n.42, s32[]{:T(128)S(6)} %select_n.46, s32[]{:T(128)S(6)} %select_n.44), kind=kLoop, calls=%fused_computation.6 | loop fusion | bytes 1572880 | tf_op jit(solution)/shard_map/dynamic_slice | solution.py:214
  29.3 2.9 %collective-permute-start = (bf16[1,128,1024]{2,1,0:T(8,128)(2,1)S(1)}, bf16[1,128,1024]{2,1,0:T(8,128)(2,1)S(1)}, u32[]{:S(2)}, u32[]{:S(2)}) collective-permute-start(bf16[1,128,1024]{2,1,0:T(8,128)(2,1)S(1)} %get-tuple-element.17), channel_id=1, source_target_pairs={{0,3},{1,0},{2,1},{3,2},{4,7},{5,4},{6,5},{7,6},{8,11},{9,8},{10,9... | collective-permute-start | bytes 786440 | tf_op jit(solution)/shard_map/ppermute | solution.py:28
  32.3 5.2 %collective-permute-start.1 = (bf16[1,128,1024]{2,1,0:T(8,128)(2,1)S(1)}, bf16[1,128,1024]{2,1,0:T(8,128)(2,1)S(1)}, u32[]{:S(2)}, u32[]{:S(2)}) collective-permute-start(bf16[1,128,1024]{2,1,0:T(8,128)(2,1)S(1)} %get-tuple-element.19), channel_id=1, source_target_pairs={{0,2},{1,3},{2,0},{3,1},{4,6},{5,7},{6,4},{7,5},{8,10},{9,11},{10,... | collective-permute-start | bytes 786440 | tf_op jit(solution)/shard_map/ppermute | solution.py:28
  37.5 2.1 %collective-permute-start.2 = (bf16[1,128,1024]{2,1,0:T(8,128)(2,1)S(1)}, bf16[1,128,1024]{2,1,0:T(8,128)(2,1)S(1)}, u32[]{:S(2)}, u32[]{:S(2)}) collective-permute-start(bf16[1,128,1024]{2,1,0:T(8,128)(2,1)S(1)} %get-tuple-element.18), channel_id=1, source_target_pairs={{0,1},{1,2},{2,3},{3,0},{4,5},{5,6},{6,7},{7,4},{8,9},{9,10},{10,1... | collective-permute-start | bytes 786440 | tf_op jit(solution)/shard_map/ppermute | solution.py:28
  39.6 2.3 %constant_dynamic-slice_fusion = bf16[4,128,1024]{2,1,0:T(8,128)(2,1)} fusion(bf16[4,512,1024]{2,1,0:T(8,128)(2,1)} %bitcast.14, s32[]{:T(128)S(6)} %select_n.48), kind=kLoop, calls=%fused_computation.3 | loop fusion | bytes 2097156 | tf_op jit(solution)/shard_map/dynamic_slice | solution.py:220
  41.9 5.2 %collective-permute-done = bf16[1,128,1024]{2,1,0:T(8,128)(2,1)S(1)} collective-permute-done((bf16[1,128,1024]{2,1,0:T(8,128)(2,1)S(1)}, bf16[1,128,1024]{2,1,0:T(8,128)(2,1)S(1)}, u32[]{:S(2)}, u32[]{:S(2)}) %collective-permute-start) | collective-permute-done | bytes 262176 | tf_op jit(solution)/shard_map/ppermute | solution.py:28
  47.1 8.6 %collective-permute-done.1 = bf16[1,128,1024]{2,1,0:T(8,128)(2,1)S(1)} collective-permute-done((bf16[1,128,1024]{2,1,0:T(8,128)(2,1)S(1)}, bf16[1,128,1024]{2,1,0:T(8,128)(2,1)S(1)}, u32[]{:S(2)}, u32[]{:S(2)}) %collective-permute-start.1) | collective-permute-done | bytes 262176 | tf_op jit(solution)/shard_map/ppermute | solution.py:28
  55.7 4.5 %collective-permute-done.2 = bf16[1,128,1024]{2,1,0:T(8,128)(2,1)S(1)} collective-permute-done((bf16[1,128,1024]{2,1,0:T(8,128)(2,1)S(1)}, bf16[1,128,1024]{2,1,0:T(8,128)(2,1)S(1)}, u32[]{:S(2)}, u32[]{:S(2)}) %collective-permute-start.2) | collective-permute-done | bytes 262176 | tf_op jit(solution)/shard_map/ppermute | solution.py:28
  60.2 0.1 pad_maximum_fusion.p0
  60.3 0.0 all-to-all-done.1
  60.3 3.5 %all-to-all-start.2 = ((bf16[4,128,1024]{2,1,0:T(8,128)(2,1)}), bf16[4,128,1024]{2,1,0:T(8,128)(2,1)S(1)}, u32[]{:S(2)}, u32[]{:S(2)}) async-start(bf16[4,128,1024]{2,1,0:T(8,128)(2,1)} %constant_dynamic-slice_fusion), calls=%async_computation.2 | async-start | bytes 2097152 | tf_op jit(solution)/shard_map/all_to_all | solution.py:222
  63.8 1.9 %collective-permute-start.3 = (bf16[64,72,128]{2,1,0:T(8,128)(2,1)S(1)}, bf16[64,72,128]{2,1,0:T(8,128)(2,1)}, u32[]{:S(2)}, u32[]{:S(2)}) collective-permute-start(bf16[64,72,128]{2,1,0:T(8,128)(2,1)S(1)} %bitcast.10), channel_id=1, source_target_pairs={{0,4},{4,0},{1,5},{5,1},{2,6},{6,2},{3,7},{7,3},{8,12},{12,8},{9,1... | collective-permute-start | bytes 3538952 | tf_op jit(solution)/shard_map/ppermute | solution.py:28
  65.8 2.4 %collective-permute-start.4 = (bf16[3,128,1024]{2,1,0:T(8,128)(2,1)S(1)}, bf16[3,128,1024]{2,1,0:T(8,128)(2,1)}, u32[]{:S(2)}, u32[]{:S(2)}) collective-permute-start(bf16[3,128,1024]{2,1,0:T(8,128)(2,1)S(1)} %pad_maximum_fusion.p0), channel_id=1, source_target_pairs={{0,128},{128,256},{256,384},{384,0},{1,129},{129,257},{257,385},{3... | collective-permute-start | bytes 2359304 | tf_op jit(solution)/shard_map/ppermute | solution.py:28
  68.2 3.5 %collective-permute-start.5 = (bf16[3,128,1024]{2,1,0:T(8,128)(2,1)S(1)}, bf16[3,128,1024]{2,1,0:T(8,128)(2,1)}, u32[]{:S(2)}, u32[]{:S(2)}) collective-permute-start(bf16[3,128,1024]{2,1,0:T(8,128)(2,1)S(1)} %pad_maximum_fusion.p0), channel_id=1, source_target_pairs={{0,384},{128,0},{256,128},{384,256},{1,385},{129,1},{257,129},{385... | collective-permute-start | bytes 2359304 | tf_op jit(solution)/shard_map/ppermute | solution.py:28
  71.6 0.1 pad_add_fusion.at_ref
  71.7 0.0 collective-permute-done.3.other_ref
  71.7 0.0 copy-done.1
  71.7 15.0 %shard_map.64 = (bf16[3,256,4096]{2,1,0:T(8,128)(2,1)}, f32[3,256,512]{2,1,0:T(8,128)}) custom-call(s32[3]{0:T(128)S(1)} %pad_add_fusion.at_ref, s32[1,4096]{1,0:T(1,128)S(1)} %bitcast.12, bf16[64,72,128]{2,1,0:T(8,128)(2,1)S(1)} %bitcast.11, bf16[64,72,128]{2,1,0:T(8,128)(2,1)} %collective-permute-done.3.other_ref, bf16[4,512,1024]{2,1,0:T(8,128)(2,1)} %bitcast.15), custom_call_target="tpu_custom_call" | custom-call | flops 1000 | bytes 1000 | tf_op jit(solution)/shard_map/pallas_call | solution.py:114
  86.7 1.0 %collective-permute-done.4.p1 = bf16[3,128,1024]{2,1,0:T(8,128)(2,1)} collective-permute-done((bf16[3,128,1024]{2,1,0:T(8,128)(2,1)S(1)}, bf16[3,128,1024]{2,1,0:T(8,128)(2,1)}, u32[]{:S(2)}, u32[]{:S(2)}) %collective-permute-start.4) | collective-permute-done | bytes 786464 | tf_op jit(solution)/shard_map/ppermute | solution.py:28
  87.7 3.3 %collective-permute-done.5.p3 = bf16[3,128,1024]{2,1,0:T(8,128)(2,1)} collective-permute-done((bf16[3,128,1024]{2,1,0:T(8,128)(2,1)S(1)}, bf16[3,128,1024]{2,1,0:T(8,128)(2,1)}, u32[]{:S(2)}, u32[]{:S(2)}) %collective-permute-start.5) | collective-permute-done | bytes 786464 | tf_op jit(solution)/shard_map/ppermute | solution.py:28
  91.0 0.0 all-to-all-done.2.p2
  91.1 6.6 %shard_map.65 = bf16[3,256,512]{2,1,0:T(8,128)(2,1)} custom-call(s32[3]{0:T(128)S(1)} %pad_add_fusion.at_ref, bf16[3,256,4096]{2,1,0:T(8,128)(2,1)} %get-tuple-element.12.s_ref, f32[3,256,512]{2,1,0:T(8,128)} %get-tuple-element.13.acc_ref, bf16[3,128,1024]{2,1,0:T(8,128)(2,1)S(1)} %pad_maximum_fusion.p0, bf16[3,128,1024]{2,1,0:T(8,128)(2,1)} %collective-permute-done.4.p1, ...), custom_call_target="tpu_custom_call" | custom-call | flops 1000 | bytes 1000 | tf_op jit(solution)/shard_map/pallas_call | solution.py:173
  (4 shorter events, 0.0 us)
Async XLA Ops:
  0.0 1.0 copy-start
  20.6 39.7 %all-to-all-start.1 = ((bf16[8,8,72,128]{3,2,1,0:T(8,128)(2,1)}), bf16[8,8,72,128]{3,2,1,0:T(8,128)(2,1)S(1)}, u32[]{:S(2)}, u32[]{:S(2)}) async-start(bf16[8,8,72,128]{3,2,1,0:T(8,128)(2,1)} %broadcast_in_dim.11), calls=%async_computation.1 | async-start | bytes 2359296 | tf_op jit(solution)/shard_map/all_to_all | solution.py:23
  28.1 43.6 %copy-start.1 = (s32[4096]{0:T(1024)S(1)}, s32[4096]{0:T(1024)}, u32[]{:S(2)}) copy-start(s32[4096]{0:T(1024)} %param.10) | copy-start | bytes 49156
  29.3 17.8 %collective-permute-start = (bf16[1,128,1024]{2,1,0:T(8,128)(2,1)S(1)}, bf16[1,128,1024]{2,1,0:T(8,128)(2,1)S(1)}, u32[]{:S(2)}, u32[]{:S(2)}) collective-permute-start(bf16[1,128,1024]{2,1,0:T(8,128)(2,1)S(1)} %get-tuple-element.17), channel_id=1, source_target_pairs={{0,3},{1,0},{2,1},{3,2},{4,7},{5,4},{6,5},{7,6},{8,11},{9,8},{10,9... | collective-permute-start | bytes 786440 | tf_op jit(solution)/shard_map/ppermute | solution.py:28
  32.3 23.4 %collective-permute-start.1 = (bf16[1,128,1024]{2,1,0:T(8,128)(2,1)S(1)}, bf16[1,128,1024]{2,1,0:T(8,128)(2,1)S(1)}, u32[]{:S(2)}, u32[]{:S(2)}) collective-permute-start(bf16[1,128,1024]{2,1,0:T(8,128)(2,1)S(1)} %get-tuple-element.19), channel_id=1, source_target_pairs={{0,2},{1,3},{2,0},{3,1},{4,6},{5,7},{6,4},{7,5},{8,10},{9,11},{10,... | collective-permute-start | bytes 786440 | tf_op jit(solution)/shard_map/ppermute | solution.py:28
  37.5 22.7 %collective-permute-start.2 = (bf16[1,128,1024]{2,1,0:T(8,128)(2,1)S(1)}, bf16[1,128,1024]{2,1,0:T(8,128)(2,1)S(1)}, u32[]{:S(2)}, u32[]{:S(2)}) collective-permute-start(bf16[1,128,1024]{2,1,0:T(8,128)(2,1)S(1)} %get-tuple-element.18), channel_id=1, source_target_pairs={{0,1},{1,2},{2,3},{3,0},{4,5},{5,6},{6,7},{7,4},{8,9},{9,10},{10,1... | collective-permute-start | bytes 786440 | tf_op jit(solution)/shard_map/ppermute | solution.py:28
  60.3 30.7 %all-to-all-start.2 = ((bf16[4,128,1024]{2,1,0:T(8,128)(2,1)}), bf16[4,128,1024]{2,1,0:T(8,128)(2,1)S(1)}, u32[]{:S(2)}, u32[]{:S(2)}) async-start(bf16[4,128,1024]{2,1,0:T(8,128)(2,1)} %constant_dynamic-slice_fusion), calls=%async_computation.2 | async-start | bytes 2097152 | tf_op jit(solution)/shard_map/all_to_all | solution.py:222
  63.8 7.9 %collective-permute-start.3 = (bf16[64,72,128]{2,1,0:T(8,128)(2,1)S(1)}, bf16[64,72,128]{2,1,0:T(8,128)(2,1)}, u32[]{:S(2)}, u32[]{:S(2)}) collective-permute-start(bf16[64,72,128]{2,1,0:T(8,128)(2,1)S(1)} %bitcast.10), channel_id=1, source_target_pairs={{0,4},{4,0},{1,5},{5,1},{2,6},{6,2},{3,7},{7,3},{8,12},{12,8},{9,1... | collective-permute-start | bytes 3538952 | tf_op jit(solution)/shard_map/ppermute | solution.py:28
  65.8 21.9 %collective-permute-start.4 = (bf16[3,128,1024]{2,1,0:T(8,128)(2,1)S(1)}, bf16[3,128,1024]{2,1,0:T(8,128)(2,1)}, u32[]{:S(2)}, u32[]{:S(2)}) collective-permute-start(bf16[3,128,1024]{2,1,0:T(8,128)(2,1)S(1)} %pad_maximum_fusion.p0), channel_id=1, source_target_pairs={{0,128},{128,256},{256,384},{384,0},{1,129},{129,257},{257,385},{3... | collective-permute-start | bytes 2359304 | tf_op jit(solution)/shard_map/ppermute | solution.py:28
  68.2 22.9 %collective-permute-start.5 = (bf16[3,128,1024]{2,1,0:T(8,128)(2,1)S(1)}, bf16[3,128,1024]{2,1,0:T(8,128)(2,1)}, u32[]{:S(2)}, u32[]{:S(2)}) collective-permute-start(bf16[3,128,1024]{2,1,0:T(8,128)(2,1)S(1)} %pad_maximum_fusion.p0), channel_id=1, source_target_pairs={{0,384},{128,0},{256,128},{384,256},{1,385},{129,1},{257,129},{385... | collective-permute-start | bytes 2359304 | tf_op jit(solution)/shard_map/ppermute | solution.py:28

commit v4 on v3

--- a/solution.py
+++ b/solution.py
@@ -28,12 +28,12 @@
     return lax.ppermute(x, axis, [(i, (i + by) % n) for i in range(n)])
 
 
-def order_kernel(at_ref, order_ref, own_ref, other_ref, rv_ref, s_out, acc_out, lt_ref, mt_ref, rhs_ref, s_buf, acc_ref, sem, out_sem):
+def order_kernel(at_ref, order_ref, own_ref, other_ref, rv_ref, s_out, acc_out, lt_ref, mt_ref, rhs_ref, s_buf, acc_ref, acc_buf, sem, out_sem):
     t = pl.program_id(0)
     last = pl.num_programs(0) - 1
     steps = rhs_ref.shape[1] // TILE
     copy = pltpu.make_async_copy(rv_ref.at[at_ref[1]], rhs_ref, sem)
-    acc_copy = pltpu.make_async_copy(acc_ref, acc_out, out_sem.at[2])
+    acc_copy = pltpu.make_async_copy(acc_buf, acc_out, out_sem.at[2])
     slot = t % 2
     s_ref = s_buf.at[slot]
 
@@ -98,6 +98,7 @@
 
     @pl.when(t == (at_ref[1] + 1) * steps - 1)
     def _():
+        acc_buf[...] = acc_ref[...].astype(jnp.bfloat16)
         acc_copy.start()
 
     @pl.when(t == last)
@@ -118,7 +119,7 @@
         out_specs=[HBM, HBM],
         out_shape=[
             pltpu.HBM((3, 2 * LANES, k), jnp.bfloat16),
-            pltpu.HBM((3, 2 * LANES, block), jnp.float32),
+            pltpu.HBM((3, 2 * LANES, block), jnp.bfloat16),
         ],
         scratch_shapes=[
             pltpu.VMEM((2 * LANES, k), jnp.bfloat16),
@@ -126,6 +127,7 @@
             pltpu.VMEM((block, group), jnp.bfloat16),
             pltpu.VMEM((2, 3, 2 * LANES, TILE), jnp.bfloat16),
             pltpu.VMEM((3, 2 * LANES, block), jnp.float32),
+            pltpu.VMEM((3, 2 * LANES, block), jnp.bfloat16),
             pltpu.SemaphoreType.DMA(()),
             pltpu.SemaphoreType.DMA((3,)),
         ],
@@ -138,48 +140,60 @@
     return pl.ds(pl.multiple_of(((d + n) % 4) * group, LANES), group)
 
 
-def contract_kernel(at_ref, s_ref, acc_ref, p0, p1, p2, p3, o_ref, rhs_ref, sum_ref, s_buf, sem):
+def contract_kernel(at_ref, s_ref, own_ref, p0, p1, p2, p3, out_ref, rhs_ref, sum_ref, own_buf, s_buf, o_buf, sem, out_sem):
     r, d = at_ref[0], at_ref[1]
     step = p0.shape[1]
     group = rhs_ref.shape[2]
+    half = 2 * step
     copies = []
     for n in (1, 2, 3):
-        at_n = [pltpu.make_async_copy(s_ref.at[:, :, lanes(d, n, group)], s_buf.at[n - 1], sem.at[5 * n - 5])]
+        at_n = []
         for t, src in enumerate((p0.at[n - 1], p1.at[n - 1], p2.at[(d + n) % 4], p3.at[n - 1])):
             rows = pl.ds(pl.multiple_of(((r - t + 4) % 4) * step, LANES), step)
-            at_n.append(pltpu.make_async_copy(src, rhs_ref.at[n - 1, rows], sem.at[5 * n - 4 + t]))
+            at_n.append(pltpu.make_async_copy(src, rhs_ref.at[n - 1, rows], sem.at[5 * n - 5 + t]))
+        at_n.append(pltpu.make_async_copy(s_ref.at[:, :, lanes(d, n, group)], s_buf.at[n - 1], sem.at[5 * n - 1]))
         copies.append(at_n)
-    copies[0].append(pltpu.make_async_copy(acc_ref, sum_ref, sem.at[15]))
+    copies[2].append(pltpu.make_async_copy(own_ref, own_buf, sem.at[15]))
     for at_n in copies:
         for copy in at_n:
             copy.start()
+    outs = []
     for n in (1, 2, 3):
         for copy in copies[n - 1]:
             copy.wait()
         for c in range(2):
-            cols = slice(c * 256, (c + 1) * 256)
+            cols = slice(c * half, (c + 1) * half)
             for m in range(3):
-                acc = sum_ref[m, :, cols] + lax.dot_general(
-                    s_buf[n - 1, m], rhs_ref[n - 1, cols, :], NT, preferred_element_type=jnp.float32
-                )
+                acc = lax.dot_general(s_buf[n - 1, m], rhs_ref[n - 1, cols, :], NT, preferred_element_type=jnp.float32)
+                if n > 1:
+                    acc += sum_ref[m, :, cols]
                 if n < 3:
                     sum_ref[m, :, cols] = acc
                 else:
-                    o_ref[m, :, cols] = acc.astype(jnp.bfloat16)
+                    o_buf[m, :, cols] = (acc + own_buf[m, :, cols].astype(jnp.float32)).astype(jnp.bfloat16)
+            if n == 3:
+                outs.append(pltpu.make_async_copy(o_buf.at[:, :, cols], out_ref.at[:, :, cols], out_sem.at[c]))
+                outs[-1].start()
+    for copy in outs:
+        copy.wait()
 
 
 def contract(at, s, summed, parts):
     group, block = parts[0].shape[2], 4 * parts[0].shape[1]
+    shape = (3, 2 * LANES, block)
     return pl.pallas_call(
         contract_kernel,
         in_specs=[SM, HBM, HBM] + [ANY] * len(parts),
-        out_specs=VM,
-        out_shape=jax.ShapeDtypeStruct((3, 2 * LANES, block), jnp.bfloat16),
+        out_specs=ANY,
+        out_shape=jax.ShapeDtypeStruct(shape, jnp.bfloat16),
         scratch_shapes=[
             pltpu.VMEM((3, block, group), jnp.bfloat16),
-            pltpu.VMEM((3, 2 * LANES, block), jnp.float32),
+            pltpu.VMEM(shape, jnp.float32),
+            pltpu.VMEM(shape, jnp.bfloat16),
             pltpu.VMEM((3, 3, 2 * LANES, group), jnp.bfloat16),
+            pltpu.VMEM(shape, jnp.bfloat16),
             pltpu.SemaphoreType.DMA((16,)),
+            pltpu.SemaphoreType.DMA((2,)),
         ],
         compiler_params=pltpu.CompilerParams(vmem_limit_bytes=20 * 2**20),
         cost_estimate=FREE,

time: 98.2 us -> 97.5 us (level)
  transfers between devices with their start and end apart: 8 -> 8, of which waited for: 5 -> 5; matrix products, arithmetic and copies ran while one was open for 4% -> 4% of each run, Pallas kernels for 15% -> 16%
where the time goes in v4:
time: 97.5 us; the launch traced here: 97 us
  starting transfers between devices  29.1 us (30%)
  waiting for transfers between devices  22.5 us (23%)
  Pallas kernels  21 us (22%)
  blocking collectives  17.6 us (18%)
  local copies, waits for them, and re-layouts  5.1 us (5%)
    ppermute x6, waiting for transfers between devices, shifted(): return lax.ppermute(x, axis, [(i, (i + by) % n) for i in range(n)])  22.5 us
    ppermute x6, starting transfers between devices, shifted(): return lax.ppermute(x, axis, [(i, (i + by) % n) for i in range(n)])  18 us
    all_to_all x1, blocking collectives, everyone(): return lax.all_to_all(jnp.broadcast_to(x[None], (n,) + x.shape), axes, 0, 0)  17.6 us
    pallas_call x1, Pallas kernels, ordered_powers(): pl.pallas_call(order_kernel, grid=(k // TILE,), in_specs=[SM, pl.BlockSpe...  15 us
    all_to_all x1, starting transfers between devices, everyone(): return lax.all_to_all(jnp.broadcast_to(x[None], (n,) + x.shape), axes, 0, 0)  7.55 us
    pallas_call x1, Pallas kernels, contract(): pl.pallas_call(contract_kernel, in_specs=[SM, HBM, HBM] + [ANY] * len(par...  5.92 us
    all_to_all x1, starting transfers between devices, on_device(): second = lax.all_to_all(second, 'depth', 0, 0)  3.53 us
    dynamic_slice x1, local copies, waits for them, and re-layouts, on_device(): lax.dynamic_slice_in_dim(rv_later, (r + 2) % n_row * quarter, quarter, 1)  2.36 us
  transfers between devices with their start and end apart: 8, of which 5 were waited for; matrix products, arithmetic and copies ran while one was open for 4% of the time, Pallas kernels for 16%

profile of v4, /device:TPU:78, one launch (start us, length us, event | category | flops | bytes accessed | tf_op | source)
XLA Modules:
  0.0 97.0 jit_solution(1564121159013107328)
XLA Ops:
  0.0 0.0 copy-start
  0.7 0.3 copy-done
  1.0 0.1 dynamic-slice_bitcast_fusion
  1.1 0.7 reduce-precision_convert_fusion
  1.7 0.1 pad_maximum_fusion.2
  1.9 17.6 %all_to_all.15 = bf16[8,72,128]{2,1,0:T(8,128)(2,1)S(1)} all-to-all(bf16[8,72,128]{2,1,0:T(8,128)(2,1)S(1)} %broadcast_in_dim.10), channel_id=1, replica_groups=mesh['row'=4,'zlo'=2,'y'=8,'core'=2,'depth'=4] {'zlo','depth'}, dimensions={0} | all-to-all | bytes 294912 | tf_op jit(solution)/shard_map/all_to_all | solution.py:23
  19.4 1.2 %broadcast_in_dim.11 = bf16[8,8,72,128]{3,2,1,0:T(8,128)(2,1)} broadcast(bf16[8,72,128]{2,1,0:T(8,128)(2,1)S(1)} %all_to_all.15), dimensions={1,2,3} | broadcast | bytes 1327104 | tf_op jit(solution)/shard_map/broadcast_in_dim | solution.py:23
  20.6 7.5 %all-to-all-start.1 = ((bf16[8,8,72,128]{3,2,1,0:T(8,128)(2,1)}), bf16[8,8,72,128]{3,2,1,0:T(8,128)(2,1)S(1)}, u32[]{:S(2)}, u32[]{:S(2)}) async-start(bf16[8,8,72,128]{3,2,1,0:T(8,128)(2,1)} %broadcast_in_dim.11), calls=%async_computation.1 | async-start | bytes 2359296 | tf_op jit(solution)/shard_map/all_to_all | solution.py:23
  28.1 0.0 copy-start.1
  28.1 1.2 %constant_dynamic-slice_fusion.3 = (bf16[1,128,1024]{2,1,0:T(8,128)(2,1)S(1)}, bf16[1,128,1024]{2,1,0:T(8,128)(2,1)S(1)}, bf16[1,128,1024]{2,1,0:T(8,128)(2,1)S(1)}) fusion(bf16[4,512,1024]{2,1,0:T(8,128)(2,1)} %bitcast.13, s32[]{:T(128)S(6)} %select_n.41, s32[]{:T(128)S(6)} %select_n.42, s32[]{:T(128)S(6)} %select_n.46, s32[]{:T(128)S(6)} %select_n.44), kind=kLoop, calls=%fused_computation.6 | loop fusion | bytes 1572880 | tf_op jit(solution)/shard_map/dynamic_slice | solution.py:228
  29.3 2.9 %collective-permute-start = (bf16[1,128,1024]{2,1,0:T(8,128)(2,1)S(1)}, bf16[1,128,1024]{2,1,0:T(8,128)(2,1)S(1)}, u32[]{:S(2)}, u32[]{:S(2)}) collective-permute-start(bf16[1,128,1024]{2,1,0:T(8,128)(2,1)S(1)} %get-tuple-element.17), channel_id=1, source_target_pairs={{0,3},{1,0},{2,1},{3,2},{4,7},{5,4},{6,5},{7,6},{8,11},{9,8},{10,9... | collective-permute-start | bytes 786440 | tf_op jit(solution)/shard_map/ppermute | solution.py:28
  32.3 5.2 %collective-permute-start.1 = (bf16[1,128,1024]{2,1,0:T(8,128)(2,1)S(1)}, bf16[1,128,1024]{2,1,0:T(8,128)(2,1)S(1)}, u32[]{:S(2)}, u32[]{:S(2)}) collective-permute-start(bf16[1,128,1024]{2,1,0:T(8,128)(2,1)S(1)} %get-tuple-element.19), channel_id=1, source_target_pairs={{0,2},{1,3},{2,0},{3,1},{4,6},{5,7},{6,4},{7,5},{8,10},{9,11},{10,... | collective-permute-start | bytes 786440 | tf_op jit(solution)/shard_map/ppermute | solution.py:28
  37.5 2.1 %collective-permute-start.2 = (bf16[1,128,1024]{2,1,0:T(8,128)(2,1)S(1)}, bf16[1,128,1024]{2,1,0:T(8,128)(2,1)S(1)}, u32[]{:S(2)}, u32[]{:S(2)}) collective-permute-start(bf16[1,128,1024]{2,1,0:T(8,128)(2,1)S(1)} %get-tuple-element.18), channel_id=1, source_target_pairs={{0,1},{1,2},{2,3},{3,0},{4,5},{5,6},{6,7},{7,4},{8,9},{9,10},{10,1... | collective-permute-start | bytes 786440 | tf_op jit(solution)/shard_map/ppermute | solution.py:28
  39.6 2.4 %constant_dynamic-slice_fusion = bf16[4,128,1024]{2,1,0:T(8,128)(2,1)} fusion(bf16[4,512,1024]{2,1,0:T(8,128)(2,1)} %bitcast.14, s32[]{:T(128)S(6)} %select_n.48), kind=kLoop, calls=%fused_computation.3 | loop fusion | bytes 2097156 | tf_op jit(solution)/shard_map/dynamic_slice | solution.py:234
  42.0 5.1 %collective-permute-done = bf16[1,128,1024]{2,1,0:T(8,128)(2,1)S(1)} collective-permute-done((bf16[1,128,1024]{2,1,0:T(8,128)(2,1)S(1)}, bf16[1,128,1024]{2,1,0:T(8,128)(2,1)S(1)}, u32[]{:S(2)}, u32[]{:S(2)}) %collective-permute-start) | collective-permute-done | bytes 262176 | tf_op jit(solution)/shard_map/ppermute | solution.py:28
  47.1 8.6 %collective-permute-done.1 = bf16[1,128,1024]{2,1,0:T(8,128)(2,1)S(1)} collective-permute-done((bf16[1,128,1024]{2,1,0:T(8,128)(2,1)S(1)}, bf16[1,128,1024]{2,1,0:T(8,128)(2,1)S(1)}, u32[]{:S(2)}, u32[]{:S(2)}) %collective-permute-start.1) | collective-permute-done | bytes 262176 | tf_op jit(solution)/shard_map/ppermute | solution.py:28
  55.7 4.5 %collective-permute-done.2 = bf16[1,128,1024]{2,1,0:T(8,128)(2,1)S(1)} collective-permute-done((bf16[1,128,1024]{2,1,0:T(8,128)(2,1)S(1)}, bf16[1,128,1024]{2,1,0:T(8,128)(2,1)S(1)}, u32[]{:S(2)}, u32[]{:S(2)}) %collective-permute-start.2) | collective-permute-done | bytes 262176 | tf_op jit(solution)/shard_map/ppermute | solution.py:28
  60.2 0.1 pad_maximum_fusion.p0
  60.3 0.0 all-to-all-done.1
  60.3 3.5 %all-to-all-start.2 = ((bf16[4,128,1024]{2,1,0:T(8,128)(2,1)}), bf16[4,128,1024]{2,1,0:T(8,128)(2,1)S(1)}, u32[]{:S(2)}, u32[]{:S(2)}) async-start(bf16[4,128,1024]{2,1,0:T(8,128)(2,1)} %constant_dynamic-slice_fusion), calls=%async_computation.2 | async-start | bytes 2097152 | tf_op jit(solution)/shard_map/all_to_all | solution.py:236
  63.8 1.9 %collective-permute-start.3 = (bf16[64,72,128]{2,1,0:T(8,128)(2,1)S(1)}, bf16[64,72,128]{2,1,0:T(8,128)(2,1)}, u32[]{:S(2)}, u32[]{:S(2)}) collective-permute-start(bf16[64,72,128]{2,1,0:T(8,128)(2,1)S(1)} %bitcast.10), channel_id=1, source_target_pairs={{0,4},{4,0},{1,5},{5,1},{2,6},{6,2},{3,7},{7,3},{8,12},{12,8},{9,1... | collective-permute-start | bytes 3538952 | tf_op jit(solution)/shard_map/ppermute | solution.py:28
  65.8 2.4 %collective-permute-start.4 = (bf16[3,128,1024]{2,1,0:T(8,128)(2,1)S(1)}, bf16[3,128,1024]{2,1,0:T(8,128)(2,1)}, u32[]{:S(2)}, u32[]{:S(2)}) collective-permute-start(bf16[3,128,1024]{2,1,0:T(8,128)(2,1)S(1)} %pad_maximum_fusion.p0), channel_id=1, source_target_pairs={{0,128},{128,256},{256,384},{384,0},{1,129},{129,257},{257,385},{3... | collective-permute-start | bytes 2359304 | tf_op jit(solution)/shard_map/ppermute | solution.py:28
  68.2 3.5 %collective-permute-start.5 = (bf16[3,128,1024]{2,1,0:T(8,128)(2,1)S(1)}, bf16[3,128,1024]{2,1,0:T(8,128)(2,1)}, u32[]{:S(2)}, u32[]{:S(2)}) collective-permute-start(bf16[3,128,1024]{2,1,0:T(8,128)(2,1)S(1)} %pad_maximum_fusion.p0), channel_id=1, source_target_pairs={{0,384},{128,0},{256,128},{384,256},{1,385},{129,1},{257,129},{385... | collective-permute-start | bytes 2359304 | tf_op jit(solution)/shard_map/ppermute | solution.py:28
  71.6 0.1 pad_add_fusion.at_ref
  71.7 0.0 collective-permute-done.3.other_ref
  71.7 0.0 copy-done.1
  71.7 15.0 %shard_map.64 = (bf16[3,256,4096]{2,1,0:T(8,128)(2,1)}, bf16[3,256,512]{2,1,0:T(8,128)(2,1)}) custom-call(s32[3]{0:T(128)S(1)} %pad_add_fusion.at_ref, s32[1,4096]{1,0:T(1,128)S(1)} %bitcast.12, bf16[64,72,128]{2,1,0:T(8,128)(2,1)S(1)} %bitcast.11, bf16[64,72,128]{2,1,0:T(8,128)(2,1)} %collective-permute-done.3.other_ref, bf16[4,512,1024]{2,1,0:T(8,128)(2,1)} %bitcast.15), custom_call_target="tpu_custom_call" | custom-call | flops 1000 | bytes 1000 | tf_op jit(solution)/shard_map/pallas_call | solution.py:115
  86.8 0.9 collective-permute-done.4.p1
  87.7 3.3 %collective-permute-done.5.p3 = bf16[3,128,1024]{2,1,0:T(8,128)(2,1)} collective-permute-done((bf16[3,128,1024]{2,1,0:T(8,128)(2,1)S(1)}, bf16[3,128,1024]{2,1,0:T(8,128)(2,1)}, u32[]{:S(2)}, u32[]{:S(2)}) %collective-permute-start.5) | collective-permute-done | bytes 786464 | tf_op jit(solution)/shard_map/ppermute | solution.py:28
  91.0 0.0 all-to-all-done.2.p2
  91.1 5.9 %shard_map.65 = bf16[3,256,512]{2,1,0:T(8,128)(2,1)} custom-call(s32[3]{0:T(128)S(1)} %pad_add_fusion.at_ref, bf16[3,256,4096]{2,1,0:T(8,128)(2,1)} %get-tuple-element.12.s_ref, bf16[3,256,512]{2,1,0:T(8,128)(2,1)} %get-tuple-element.13.own_ref, bf16[3,128,1024]{2,1,0:T(8,128)(2,1)S(1)} %pad_maximum_fusion.p0, ...), custom_call_target="tpu_custom_call" | custom-call | flops 1000 | bytes 1000 | tf_op jit(solution)/shard_map/pallas_call | solution.py:184
  (4 shorter events, 0.0 us)
Async XLA Ops:
  0.0 1.0 copy-start
  20.6 39.7 %all-to-all-start.1 = ((bf16[8,8,72,128]{3,2,1,0:T(8,128)(2,1)}), bf16[8,8,72,128]{3,2,1,0:T(8,128)(2,1)S(1)}, u32[]{:S(2)}, u32[]{:S(2)}) async-start(bf16[8,8,72,128]{3,2,1,0:T(8,128)(2,1)} %broadcast_in_dim.11), calls=%async_computation.1 | async-start | bytes 2359296 | tf_op jit(solution)/shard_map/all_to_all | solution.py:23
  28.1 43.6 %copy-start.1 = (s32[4096]{0:T(1024)S(1)}, s32[4096]{0:T(1024)}, u32[]{:S(2)}) copy-start(s32[4096]{0:T(1024)} %param.10) | copy-start | bytes 49156
  29.3 17.8 %collective-permute-start = (bf16[1,128,1024]{2,1,0:T(8,128)(2,1)S(1)}, bf16[1,128,1024]{2,1,0:T(8,128)(2,1)S(1)}, u32[]{:S(2)}, u32[]{:S(2)}) collective-permute-start(bf16[1,128,1024]{2,1,0:T(8,128)(2,1)S(1)} %get-tuple-element.17), channel_id=1, source_target_pairs={{0,3},{1,0},{2,1},{3,2},{4,7},{5,4},{6,5},{7,6},{8,11},{9,8},{10,9... | collective-permute-start | bytes 786440 | tf_op jit(solution)/shard_map/ppermute | solution.py:28
  32.3 23.4 %collective-permute-start.1 = (bf16[1,128,1024]{2,1,0:T(8,128)(2,1)S(1)}, bf16[1,128,1024]{2,1,0:T(8,128)(2,1)S(1)}, u32[]{:S(2)}, u32[]{:S(2)}) collective-permute-start(bf16[1,128,1024]{2,1,0:T(8,128)(2,1)S(1)} %get-tuple-element.19), channel_id=1, source_target_pairs={{0,2},{1,3},{2,0},{3,1},{4,6},{5,7},{6,4},{7,5},{8,10},{9,11},{10,... | collective-permute-start | bytes 786440 | tf_op jit(solution)/shard_map/ppermute | solution.py:28
  37.5 22.7 %collective-permute-start.2 = (bf16[1,128,1024]{2,1,0:T(8,128)(2,1)S(1)}, bf16[1,128,1024]{2,1,0:T(8,128)(2,1)S(1)}, u32[]{:S(2)}, u32[]{:S(2)}) collective-permute-start(bf16[1,128,1024]{2,1,0:T(8,128)(2,1)S(1)} %get-tuple-element.18), channel_id=1, source_target_pairs={{0,1},{1,2},{2,3},{3,0},{4,5},{5,6},{6,7},{7,4},{8,9},{9,10},{10,1... | collective-permute-start | bytes 786440 | tf_op jit(solution)/shard_map/ppermute | solution.py:28
  60.3 30.7 %all-to-all-start.2 = ((bf16[4,128,1024]{2,1,0:T(8,128)(2,1)}), bf16[4,128,1024]{2,1,0:T(8,128)(2,1)S(1)}, u32[]{:S(2)}, u32[]{:S(2)}) async-start(bf16[4,128,1024]{2,1,0:T(8,128)(2,1)} %constant_dynamic-slice_fusion), calls=%async_computation.2 | async-start | bytes 2097152 | tf_op jit(solution)/shard_map/all_to_all | solution.py:236
  63.8 7.9 %collective-permute-start.3 = (bf16[64,72,128]{2,1,0:T(8,128)(2,1)S(1)}, bf16[64,72,128]{2,1,0:T(8,128)(2,1)}, u32[]{:S(2)}, u32[]{:S(2)}) collective-permute-start(bf16[64,72,128]{2,1,0:T(8,128)(2,1)S(1)} %bitcast.10), channel_id=1, source_target_pairs={{0,4},{4,0},{1,5},{5,1},{2,6},{6,2},{3,7},{7,3},{8,12},{12,8},{9,1... | collective-permute-start | bytes 3538952 | tf_op jit(solution)/shard_map/ppermute | solution.py:28
  65.8 21.9 %collective-permute-start.4 = (bf16[3,128,1024]{2,1,0:T(8,128)(2,1)S(1)}, bf16[3,128,1024]{2,1,0:T(8,128)(2,1)}, u32[]{:S(2)}, u32[]{:S(2)}) collective-permute-start(bf16[3,128,1024]{2,1,0:T(8,128)(2,1)S(1)} %pad_maximum_fusion.p0), channel_id=1, source_target_pairs={{0,128},{128,256},{256,384},{384,0},{1,129},{129,257},{257,385},{3... | collective-permute-start | bytes 2359304 | tf_op jit(solution)/shard_map/ppermute | solution.py:28
  68.2 22.9 %collective-permute-start.5 = (bf16[3,128,1024]{2,1,0:T(8,128)(2,1)S(1)}, bf16[3,128,1024]{2,1,0:T(8,128)(2,1)}, u32[]{:S(2)}, u32[]{:S(2)}) collective-permute-start(bf16[3,128,1024]{2,1,0:T(8,128)(2,1)S(1)} %pad_maximum_fusion.p0), channel_id=1, source_target_pairs={{0,384},{128,0},{256,128},{384,256},{1,385},{129,1},{257,129},{385... | collective-permute-start | bytes 2359304 | tf_op jit(solution)/shard_map/ppermute | solution.py:28

commit v5 on v4

--- a/solution.py
+++ b/solution.py
@@ -47,11 +47,12 @@
         for h, src in enumerate((own_ref, other_ref)):
             for q in range(16):
                 for a in range(2):
-                    blk = src[4 * q:4 * q + 4, a * WIDTH:(a + 1) * WIDTH, :].reshape(LANES, LANES)
+                    rows = src[q // 2, (q % 2) * 256:(q % 2 + 1) * 256, :].reshape(4, 2 * WIDTH, LANES)
+                    blk = rows[:, a * WIDTH:(a + 1) * WIDTH, :].reshape(LANES, LANES)
                     at = (16 * h + q) * LANES
                     lt_ref[a * LANES:(a + 1) * LANES, at:at + LANES] = blk.T
-        mt = jnp.concatenate([own_ref[:, 2 * WIDTH, :], other_ref[:, 2 * WIDTH, :]], axis=0)
-        mt_ref[...] = mt.astype(jnp.float32).T.astype(jnp.bfloat16)
+        mt = jnp.concatenate([ref[:, 512:, :].astype(jnp.float32).reshape(64, LANES) for ref in (own_ref, other_ref)], axis=0)
+        mt_ref[...] = mt.T.astype(jnp.bfloat16)
 
     e = order_ref[...]
     j = e & 31
@@ -142,58 +143,60 @@
 
 def contract_kernel(at_ref, s_ref, own_ref, p0, p1, p2, p3, out_ref, rhs_ref, sum_ref, own_buf, s_buf, o_buf, sem, out_sem):
     r, d = at_ref[0], at_ref[1]
-    step = p0.shape[1]
-    group = rhs_ref.shape[2]
+    step, group = p0.shape[1], p0.shape[2]
     half = 2 * step
+    quarters = ((r, (r + 2) % 4), ((r + 3) % 4, (r + 1) % 4))
     copies = []
     for n in (1, 2, 3):
-        at_n = []
-        for t, src in enumerate((p0.at[n - 1], p1.at[n - 1], p2.at[(d + n) % 4], p3.at[n - 1])):
-            rows = pl.ds(pl.multiple_of(((r - t + 4) % 4) * step, LANES), step)
-            at_n.append(pltpu.make_async_copy(src, rhs_ref.at[n - 1, rows], sem.at[5 * n - 5 + t]))
-        at_n.append(pltpu.make_async_copy(s_ref.at[:, :, lanes(d, n, group)], s_buf.at[n - 1], sem.at[5 * n - 1]))
-        copies.append(at_n)
-    copies[2].append(pltpu.make_async_copy(own_ref, own_buf, sem.at[15]))
-    for at_n in copies:
-        for copy in at_n:
-            copy.start()
+        copies.append(pltpu.make_async_copy(s_ref.at[:, :, lanes(d, n, group)], s_buf.at[n - 1], sem.at[3 * n - 3]))
+        copies.append(pltpu.make_async_copy(p1.at[n - 1], rhs_ref.at[n - 1, :step], sem.at[3 * n - 2]))
+        copies.append(pltpu.make_async_copy(p3.at[n - 1], rhs_ref.at[n - 1, step:], sem.at[3 * n - 1]))
+    copies.append(pltpu.make_async_copy(own_ref, own_buf, sem.at[9]))
+    for copy in copies:
+        copy.start()
     outs = []
     for n in (1, 2, 3):
-        for copy in copies[n - 1]:
+        for copy in copies[3 * n - 3:3 * n]:
             copy.wait()
-        for c in range(2):
-            cols = slice(c * half, (c + 1) * half)
-            for m in range(3):
-                acc = lax.dot_general(s_buf[n - 1, m], rhs_ref[n - 1, cols, :], NT, preferred_element_type=jnp.float32)
+        if n == 3:
+            copies[9].wait()
+        rhs = (jnp.concatenate([p0[n - 1], p2[(d + n) % 4]], axis=0), rhs_ref[n - 1])
+        for m in range(3):
+            for c in range(2):
+                cols = slice(c * half, (c + 1) * half)
+                acc = lax.dot_general(s_buf[n - 1, m], rhs[c], NT, preferred_element_type=jnp.float32)
                 if n > 1:
                     acc += sum_ref[m, :, cols]
                 if n < 3:
                     sum_ref[m, :, cols] = acc
-                else:
-                    o_buf[m, :, cols] = (acc + own_buf[m, :, cols].astype(jnp.float32)).astype(jnp.bfloat16)
+                    continue
+                for a, q in enumerate(quarters[c]):
+                    at = pl.ds(pl.multiple_of(q * step, LANES), step)
+                    own = own_buf[m, :, at].astype(jnp.float32)
+                    o_buf[m, :, at] = (acc[:, a * step:(a + 1) * step] + own).astype(jnp.bfloat16)
             if n == 3:
-                outs.append(pltpu.make_async_copy(o_buf.at[:, :, cols], out_ref.at[:, :, cols], out_sem.at[c]))
+                outs.append(pltpu.make_async_copy(o_buf.at[m], out_ref.at[m], out_sem.at[m]))
                 outs[-1].start()
     for copy in outs:
         copy.wait()
 
 
 def contract(at, s, summed, parts):
-    group, block = parts[0].shape[2], 4 * parts[0].shape[1]
-    shape = (3, 2 * LANES, block)
+    step, group = parts[0].shape[1], parts[0].shape[2]
+    shape = (3, 2 * LANES, 4 * step)
     return pl.pallas_call(
         contract_kernel,
-        in_specs=[SM, HBM, HBM] + [ANY] * len(parts),
+        in_specs=[SM, HBM, HBM, VM, ANY, VM, ANY],
         out_specs=ANY,
         out_shape=jax.ShapeDtypeStruct(shape, jnp.bfloat16),
         scratch_shapes=[
-            pltpu.VMEM((3, block, group), jnp.bfloat16),
+            pltpu.VMEM((3, 2 * step, group), jnp.bfloat16),
             pltpu.VMEM(shape, jnp.float32),
             pltpu.VMEM(shape, jnp.bfloat16),
             pltpu.VMEM((3, 3, 2 * LANES, group), jnp.bfloat16),
             pltpu.VMEM(shape, jnp.bfloat16),
-            pltpu.SemaphoreType.DMA((16,)),
-            pltpu.SemaphoreType.DMA((2,)),
+            pltpu.SemaphoreType.DMA((10,)),
+            pltpu.SemaphoreType.DMA((3,)),
         ],
         compiler_params=pltpu.CompilerParams(vmem_limit_bytes=20 * 2**20),
         cost_estimate=FREE,
@@ -220,7 +223,8 @@
     scal = jnp.broadcast_to(scal[None], (8, LANES))
     mine = jnp.concatenate([mine[:, :LANES], mine[:, LANES:], scal], axis=0)
     by_z = everyone(mine, ("zlo", "depth"))
-    same = everyone(by_z, "y").reshape(64, 72, LANES)
+    by_z = jnp.concatenate([by_z[:, :2 * WIDTH].reshape(-1, LANES), by_z[:, 2 * WIDTH]])
+    same = everyone(by_z, "y")
 
     rv = right_vectors.reshape(n_depth, block, group)
 

time: 97.5 us -> 97.4 us (level)
  transfers between devices with their start and end apart: 8 -> 8, of which waited for: 5 -> 5; matrix products, arithmetic and copies ran while one was open for 4% -> 4% of each run, Pallas kernels for 16% -> 15%
where the time goes in v5:
time: 97.4 us; the launch traced here: 96.9 us
  starting transfers between devices  29.1 us (30%)
  waiting for transfers between devices  22.5 us (23%)
  Pallas kernels  20.9 us (21%)
  blocking collectives  17.6 us (18%)
  local copies, waits for them, and re-layouts  5.04 us (5%)
    ppermute x6, waiting for transfers between devices, shifted(): return lax.ppermute(x, axis, [(i, (i + by) % n) for i in range(n)])  22.5 us
    ppermute x6, starting transfers between devices, shifted(): return lax.ppermute(x, axis, [(i, (i + by) % n) for i in range(n)])  18 us
    all_to_all x1, blocking collectives, everyone(): return lax.all_to_all(jnp.broadcast_to(x[None], (n,) + x.shape), axes, 0, 0)  17.6 us
    pallas_call x1, Pallas kernels, ordered_powers(): pl.pallas_call(order_kernel, grid=(k // TILE,), in_specs=[SM, pl.BlockSpe...  15 us
    all_to_all x1, starting transfers between devices, everyone(): return lax.all_to_all(jnp.broadcast_to(x[None], (n,) + x.shape), axes, 0, 0)  7.55 us
    pallas_call x1, Pallas kernels, contract(): pl.pallas_call(contract_kernel, in_specs=[SM, HBM, HBM, VM, ANY, VM, ANY]...  5.86 us
    all_to_all x1, starting transfers between devices, on_device(): second = lax.all_to_all(second, 'depth', 0, 0)  3.53 us
    dynamic_slice x1, local copies, waits for them, and re-layouts, on_device(): lax.dynamic_slice_in_dim(rv_later, (r + 2) % n_row * quarter, quarter, 1)  2.34 us
  transfers between devices with their start and end apart: 8, of which 5 were waited for; matrix products, arithmetic and copies ran while one was open for 4% of the time, Pallas kernels for 15%

profile of v5, /device:TPU:78, one launch (start us, length us, event | category | flops | bytes accessed | tf_op | source)
XLA Modules:
  0.0 96.9 jit_solution(14345833842757676172)
XLA Ops:
  0.0 0.0 copy-start
  0.7 0.3 copy-done
  1.0 0.1 dynamic-slice_bitcast_fusion
  1.1 0.7 reduce-precision_convert_fusion
  1.7 0.1 pad_maximum_fusion.3
  1.9 17.6 %all_to_all.15 = bf16[8,72,128]{2,1,0:T(8,128)(2,1)S(1)} all-to-all(bf16[8,72,128]{2,1,0:T(8,128)(2,1)S(1)} %broadcast_in_dim.10), channel_id=1, replica_groups=mesh['row'=4,'zlo'=2,'y'=8,'core'=2,'depth'=4] {'zlo','depth'}, dimensions={0} | all-to-all | bytes 294912 | tf_op jit(solution)/shard_map/all_to_all | solution.py:23
  19.5 1.1 %broadcast_in_dim.11 = bf16[8,520,128]{2,1,0:T(8,128)(2,1)} broadcast(bf16[520,128]{1,0:T(8,128)(2,1)S(1)} %pad_maximum_fusion.1), dimensions={1,2} | broadcast | bytes 1198080 | tf_op jit(solution)/shard_map/broadcast_in_dim | solution.py:23
  20.6 7.5 %all-to-all-start.1 = ((bf16[8,520,128]{2,1,0:T(8,128)(2,1)}), bf16[8,520,128]{2,1,0:T(8,128)(2,1)S(1)}, u32[]{:S(2)}, u32[]{:S(2)}) async-start(bf16[8,520,128]{2,1,0:T(8,128)(2,1)} %broadcast_in_dim.11), calls=%async_computation.1 | async-start | bytes 2129920 | tf_op jit(solution)/shard_map/all_to_all | solution.py:23
  28.1 0.0 copy-start.1
  28.1 1.2 %constant_dynamic-slice_fusion.3 = (bf16[1,128,1024]{2,1,0:T(8,128)(2,1)S(1)}, bf16[1,128,1024]{2,1,0:T(8,128)(2,1)S(1)}, bf16[1,128,1024]{2,1,0:T(8,128)(2,1)S(1)}) fusion(bf16[4,512,1024]{2,1,0:T(8,128)(2,1)} %bitcast.14, s32[]{:T(128)S(6)} %select_n.41, s32[]{:T(128)S(6)} %select_n.42, s32[]{:T(128)S(6)} %select_n.46, s32[]{:T(128)S(6)} %select_n.44), kind=kLoop, calls=%fused_computation.8 | loop fusion | bytes 1572880 | tf_op jit(solution)/shard_map/dynamic_slice | solution.py:232
  29.3 2.9 %collective-permute-start = (bf16[1,128,1024]{2,1,0:T(8,128)(2,1)S(1)}, bf16[1,128,1024]{2,1,0:T(8,128)(2,1)S(1)}, u32[]{:S(2)}, u32[]{:S(2)}) collective-permute-start(bf16[1,128,1024]{2,1,0:T(8,128)(2,1)S(1)} %get-tuple-element.17), channel_id=1, source_target_pairs={{0,3},{1,0},{2,1},{3,2},{4,7},{5,4},{6,5},{7,6},{8,11},{9,8},{10,9... | collective-permute-start | bytes 786440 | tf_op jit(solution)/shard_map/ppermute | solution.py:28
  32.3 5.2 %collective-permute-start.1 = (bf16[1,128,1024]{2,1,0:T(8,128)(2,1)S(1)}, bf16[1,128,1024]{2,1,0:T(8,128)(2,1)S(1)}, u32[]{:S(2)}, u32[]{:S(2)}) collective-permute-start(bf16[1,128,1024]{2,1,0:T(8,128)(2,1)S(1)} %get-tuple-element.19), channel_id=1, source_target_pairs={{0,2},{1,3},{2,0},{3,1},{4,6},{5,7},{6,4},{7,5},{8,10},{9,11},{10,... | collective-permute-start | bytes 786440 | tf_op jit(solution)/shard_map/ppermute | solution.py:28
  37.5 2.1 %collective-permute-start.2 = (bf16[1,128,1024]{2,1,0:T(8,128)(2,1)S(1)}, bf16[1,128,1024]{2,1,0:T(8,128)(2,1)S(1)}, u32[]{:S(2)}, u32[]{:S(2)}) collective-permute-start(bf16[1,128,1024]{2,1,0:T(8,128)(2,1)S(1)} %get-tuple-element.18), channel_id=1, source_target_pairs={{0,1},{1,2},{2,3},{3,0},{4,5},{5,6},{6,7},{7,4},{8,9},{9,10},{10,1... | collective-permute-start | bytes 786440 | tf_op jit(solution)/shard_map/ppermute | solution.py:28
  39.6 2.3 %constant_dynamic-slice_fusion = bf16[4,128,1024]{2,1,0:T(8,128)(2,1)} fusion(bf16[4,512,1024]{2,1,0:T(8,128)(2,1)} %bitcast.15, s32[]{:T(128)S(6)} %select_n.48), kind=kLoop, calls=%fused_computation.5 | loop fusion | bytes 2097156 | tf_op jit(solution)/shard_map/dynamic_slice | solution.py:238
  42.0 5.1 %collective-permute-done = bf16[1,128,1024]{2,1,0:T(8,128)(2,1)S(1)} collective-permute-done((bf16[1,128,1024]{2,1,0:T(8,128)(2,1)S(1)}, bf16[1,128,1024]{2,1,0:T(8,128)(2,1)S(1)}, u32[]{:S(2)}, u32[]{:S(2)}) %collective-permute-start) | collective-permute-done | bytes 262176 | tf_op jit(solution)/shard_map/ppermute | solution.py:28
  47.1 8.6 %collective-permute-done.1 = bf16[1,128,1024]{2,1,0:T(8,128)(2,1)S(1)} collective-permute-done((bf16[1,128,1024]{2,1,0:T(8,128)(2,1)S(1)}, bf16[1,128,1024]{2,1,0:T(8,128)(2,1)S(1)}, u32[]{:S(2)}, u32[]{:S(2)}) %collective-permute-start.1) | collective-permute-done | bytes 262176 | tf_op jit(solution)/shard_map/ppermute | solution.py:28
  55.7 4.5 %collective-permute-done.2 = bf16[1,128,1024]{2,1,0:T(8,128)(2,1)S(1)} collective-permute-done((bf16[1,128,1024]{2,1,0:T(8,128)(2,1)S(1)}, bf16[1,128,1024]{2,1,0:T(8,128)(2,1)S(1)}, u32[]{:S(2)}, u32[]{:S(2)}) %collective-permute-start.2) | collective-permute-done | bytes 262176 | tf_op jit(solution)/shard_map/ppermute | solution.py:28
  60.2 0.1 pad_maximum_fusion.p0
  60.3 0.0 all-to-all-done.1.own_ref
  60.3 3.5 %all-to-all-start.2 = ((bf16[4,128,1024]{2,1,0:T(8,128)(2,1)}), bf16[4,128,1024]{2,1,0:T(8,128)(2,1)S(1)}, u32[]{:S(2)}, u32[]{:S(2)}) async-start(bf16[4,128,1024]{2,1,0:T(8,128)(2,1)} %constant_dynamic-slice_fusion), calls=%async_computation.2 | async-start | bytes 2097152 | tf_op jit(solution)/shard_map/all_to_all | solution.py:240
  63.8 1.9 %collective-permute-start.3 = (bf16[8,520,128]{2,1,0:T(8,128)(2,1)S(1)}, bf16[8,520,128]{2,1,0:T(8,128)(2,1)}, u32[]{:S(2)}, u32[]{:S(2)}) collective-permute-start(bf16[8,520,128]{2,1,0:T(8,128)(2,1)S(1)} %all-to-all-done.1.own_ref), channel_id=1, source_target_pairs={{0,4},{4,0},{1,5},{5,1},{2,6},{6,2},{3,7},{7,3},{8,12},{12,8},{9,1... | collective-permute-start | bytes 3194888 | tf_op jit(solution)/shard_map/ppermute | solution.py:28
  65.8 2.4 %collective-permute-start.4 = (bf16[3,128,1024]{2,1,0:T(8,128)(2,1)S(1)}, bf16[3,128,1024]{2,1,0:T(8,128)(2,1)}, u32[]{:S(2)}, u32[]{:S(2)}) collective-permute-start(bf16[3,128,1024]{2,1,0:T(8,128)(2,1)S(1)} %pad_maximum_fusion.p0), channel_id=1, source_target_pairs={{0,128},{128,256},{256,384},{384,0},{1,129},{129,257},{257,385},{3... | collective-permute-start | bytes 2359304 | tf_op jit(solution)/shard_map/ppermute | solution.py:28
  68.2 3.5 %collective-permute-start.5 = (bf16[3,128,1024]{2,1,0:T(8,128)(2,1)S(1)}, bf16[3,128,1024]{2,1,0:T(8,128)(2,1)}, u32[]{:S(2)}, u32[]{:S(2)}) collective-permute-start(bf16[3,128,1024]{2,1,0:T(8,128)(2,1)S(1)} %pad_maximum_fusion.p0), channel_id=1, source_target_pairs={{0,384},{128,0},{256,128},{384,256},{1,385},{129,1},{257,129},{385... | collective-permute-start | bytes 2359304 | tf_op jit(solution)/shard_map/ppermute | solution.py:28
  71.6 0.1 pad_add_fusion.at_ref
  71.7 0.0 collective-permute-done.3.other_ref
  71.7 0.0 copy-done.1
  71.7 15.0 %shard_map.64 = (bf16[3,256,4096]{2,1,0:T(8,128)(2,1)}, bf16[3,256,512]{2,1,0:T(8,128)(2,1)}) custom-call(s32[3]{0:T(128)S(1)} %pad_add_fusion.at_ref, s32[1,4096]{1,0:T(1,128)S(1)} %bitcast.13, bf16[8,520,128]{2,1,0:T(8,128)(2,1)S(1)} %all-to-all-done.1.own_ref, bf16[8,520,128]{2,1,0:T(8,128)(2,1)} %collective-permute-done.3.other_ref, ...), custom_call_target="tpu_custom_call" | custom-call | flops 1000 | bytes 1000 | tf_op jit(solution)/shard_map/pallas_call | solution.py:116
  86.7 1.0 %collective-permute-done.4.p1 = bf16[3,128,1024]{2,1,0:T(8,128)(2,1)} collective-permute-done((bf16[3,128,1024]{2,1,0:T(8,128)(2,1)S(1)}, bf16[3,128,1024]{2,1,0:T(8,128)(2,1)}, u32[]{:S(2)}, u32[]{:S(2)}) %collective-permute-start.4) | collective-permute-done | bytes 786464 | tf_op jit(solution)/shard_map/ppermute | solution.py:28
  87.7 3.3 %collective-permute-done.5.p3 = bf16[3,128,1024]{2,1,0:T(8,128)(2,1)} collective-permute-done((bf16[3,128,1024]{2,1,0:T(8,128)(2,1)S(1)}, bf16[3,128,1024]{2,1,0:T(8,128)(2,1)}, u32[]{:S(2)}, u32[]{:S(2)}) %collective-permute-start.5) | collective-permute-done | bytes 786464 | tf_op jit(solution)/shard_map/ppermute | solution.py:28
  91.0 0.0 all-to-all-done.2.p2
  91.0 5.9 %shard_map.65 = bf16[3,256,512]{2,1,0:T(8,128)(2,1)} custom-call(s32[3]{0:T(128)S(1)} %pad_add_fusion.at_ref, bf16[3,256,4096]{2,1,0:T(8,128)(2,1)} %get-tuple-element.12.s_ref, bf16[3,256,512]{2,1,0:T(8,128)(2,1)} %get-tuple-element.13.own_ref, bf16[3,128,1024]{2,1,0:T(8,128)(2,1)S(1)} %pad_maximum_fusion.p0, ...), custom_call_target="tpu_custom_call" | custom-call | flops 1000 | bytes 1000 | tf_op jit(solution)/shard_map/pallas_call | solution.py:187
  (8 shorter events, 0.1 us)
Async XLA Ops:
  0.0 1.0 copy-start
  20.6 39.7 %all-to-all-start.1 = ((bf16[8,520,128]{2,1,0:T(8,128)(2,1)}), bf16[8,520,128]{2,1,0:T(8,128)(2,1)S(1)}, u32[]{:S(2)}, u32[]{:S(2)}) async-start(bf16[8,520,128]{2,1,0:T(8,128)(2,1)} %broadcast_in_dim.11), calls=%async_computation.1 | async-start | bytes 2129920 | tf_op jit(solution)/shard_map/all_to_all | solution.py:23
  28.1 43.6 %copy-start.1 = (s32[4096]{0:T(1024)S(1)}, s32[4096]{0:T(1024)}, u32[]{:S(2)}) copy-start(s32[4096]{0:T(1024)} %param.10) | copy-start | bytes 49156
  29.3 17.8 %collective-permute-start = (bf16[1,128,1024]{2,1,0:T(8,128)(2,1)S(1)}, bf16[1,128,1024]{2,1,0:T(8,128)(2,1)S(1)}, u32[]{:S(2)}, u32[]{:S(2)}) collective-permute-start(bf16[1,128,1024]{2,1,0:T(8,128)(2,1)S(1)} %get-tuple-element.17), channel_id=1, source_target_pairs={{0,3},{1,0},{2,1},{3,2},{4,7},{5,4},{6,5},{7,6},{8,11},{9,8},{10,9... | collective-permute-start | bytes 786440 | tf_op jit(solution)/shard_map/ppermute | solution.py:28
  32.3 23.4 %collective-permute-start.1 = (bf16[1,128,1024]{2,1,0:T(8,128)(2,1)S(1)}, bf16[1,128,1024]{2,1,0:T(8,128)(2,1)S(1)}, u32[]{:S(2)}, u32[]{:S(2)}) collective-permute-start(bf16[1,128,1024]{2,1,0:T(8,128)(2,1)S(1)} %get-tuple-element.19), channel_id=1, source_target_pairs={{0,2},{1,3},{2,0},{3,1},{4,6},{5,7},{6,4},{7,5},{8,10},{9,11},{10,... | collective-permute-start | bytes 786440 | tf_op jit(solution)/shard_map/ppermute | solution.py:28
  37.5 22.7 %collective-permute-start.2 = (bf16[1,128,1024]{2,1,0:T(8,128)(2,1)S(1)}, bf16[1,128,1024]{2,1,0:T(8,128)(2,1)S(1)}, u32[]{:S(2)}, u32[]{:S(2)}) collective-permute-start(bf16[1,128,1024]{2,1,0:T(8,128)(2,1)S(1)} %get-tuple-element.18), channel_id=1, source_target_pairs={{0,1},{1,2},{2,3},{3,0},{4,5},{5,6},{6,7},{7,4},{8,9},{9,10},{10,1... | collective-permute-start | bytes 786440 | tf_op jit(solution)/shard_map/ppermute | solution.py:28
  60.3 30.7 %all-to-all-start.2 = ((bf16[4,128,1024]{2,1,0:T(8,128)(2,1)}), bf16[4,128,1024]{2,1,0:T(8,128)(2,1)S(1)}, u32[]{:S(2)}, u32[]{:S(2)}) async-start(bf16[4,128,1024]{2,1,0:T(8,128)(2,1)} %constant_dynamic-slice_fusion), calls=%async_computation.2 | async-start | bytes 2097152 | tf_op jit(solution)/shard_map/all_to_all | solution.py:240
  63.8 7.9 %collective-permute-start.3 = (bf16[8,520,128]{2,1,0:T(8,128)(2,1)S(1)}, bf16[8,520,128]{2,1,0:T(8,128)(2,1)}, u32[]{:S(2)}, u32[]{:S(2)}) collective-permute-start(bf16[8,520,128]{2,1,0:T(8,128)(2,1)S(1)} %all-to-all-done.1.own_ref), channel_id=1, source_target_pairs={{0,4},{4,0},{1,5},{5,1},{2,6},{6,2},{3,7},{7,3},{8,12},{12,8},{9,1... | collective-permute-start | bytes 3194888 | tf_op jit(solution)/shard_map/ppermute | solution.py:28
  65.8 21.9 %collective-permute-start.4 = (bf16[3,128,1024]{2,1,0:T(8,128)(2,1)S(1)}, bf16[3,128,1024]{2,1,0:T(8,128)(2,1)}, u32[]{:S(2)}, u32[]{:S(2)}) collective-permute-start(bf16[3,128,1024]{2,1,0:T(8,128)(2,1)S(1)} %pad_maximum_fusion.p0), channel_id=1, source_target_pairs={{0,128},{128,256},{256,384},{384,0},{1,129},{129,257},{257,385},{3... | collective-permute-start | bytes 2359304 | tf_op jit(solution)/shard_map/ppermute | solution.py:28
  68.2 22.9 %collective-permute-start.5 = (bf16[3,128,1024]{2,1,0:T(8,128)(2,1)S(1)}, bf16[3,128,1024]{2,1,0:T(8,128)(2,1)}, u32[]{:S(2)}, u32[]{:S(2)}) collective-permute-start(bf16[3,128,1024]{2,1,0:T(8,128)(2,1)S(1)} %pad_maximum_fusion.p0), channel_id=1, source_target_pairs={{0,384},{128,0},{256,128},{384,256},{1,385},{129,1},{257,129},{385... | collective-permute-start | bytes 2359304 | tf_op jit(solution)/shard_map/ppermute | solution.py:28
